TPU v7x, 32 devices: a whole 2x2x4 slice. The times are simulated.
32 devices in a mesh: grp: 4 (over y, x), lon: 8 (over z, core).
Axes of the slice: x: 2, y: 2, z: 4, core: 2. Of those that a mesh axis runs over, the one named last changes fastest.
Arguments:
- surface_temp: float32 [256, 8192], P('grp', 'lon'), may hold values from -1.9 to 0.6
- salinity: float32 [256, 8192], P('grp', 'lon'), may hold values from 30 to 35
- wind_stress: float32 [2, 256, 8192], P(None, 'grp', 'lon'), may hold values from -6 to 6
- ocean_current: float32 [2, 256, 8192], P(None, 'grp', 'lon'), may hold values from -3 to 3
- velocity: float32 [2, 256, 8192], P(None, 'grp', 'lon'), may hold values from -3 to 3
- stress: float32 [3, 256, 8192], P(None, 'grp', 'lon'), may hold values from -3 to 3
- ice_area: float32 [1024, 5, 2048], P(('grp', 'lon')), may hold values from 0.13 to 0.2
- ice_volume: float32 [1024, 5, 2048], P(('grp', 'lon')), may hold values from 0.1 to 1.5
- air_temp: float32 [1024, 2048], P(('grp', 'lon')), may hold values from -30 to -5
- ice_mask: int32 [1024], P(('grp', 'lon')), may hold values 0 or 1
- curve_pos: int32 [1024], P(('grp', 'lon')), may hold values from 0 to 255, as said below
Outputs:
- velocity_out: float32 [2, 256, 8192], P(None, 'grp', 'lon')
- stress_out: float32 [3, 256, 8192], P(None, 'grp', 'lon')
- area_out: float32 [1024, 5, 2048], P(('grp', 'lon'))
- volume_out: float32 [1024, 5, 2048], P(('grp', 'lon'))
Inputs may be any that keep to these rules, and one draw needn't show every extreme that they name: `curve_pos`: each band's curve holds each position once; ice device j of a band holds positions j * 32 to (j + 1) * 32 - 1; from one tile to one ice device go at most 8 blocks, and exactly 8 for some pairs.
All inputs are finite; a program needn't handle non-finite values. No bound on the sum of `ice_mask` on one device may be relied on, other than what follows from the above.
Results may differ from a plain program's by a relative error of at most 0.000025.
Values sent between devices are 32-bit elements; how exact they have to be, the bound alone decides.
A program may use at most 64 MiB of HBM per device.

v0:
```python
import jax
import jax.numpy as jnp
from jax import lax
from jax.sharding import PartitionSpec as P

BY = 8
BX = 256
SUB = 4


KAPPA = 0.02
MELT = 0.6
PSTAR = 10.0
CSTAR = 20.0
RELAX = 0.4
ECC2 = 4.0
DMIN2 = 0.01
DTE = 0.5
DRAG = 1.0
FCOR = 0.3


def swapped(block, axis, stride):
    count = lax.axis_size(axis)
    route = []
    for low in range(count):
        high = low | 1 << stride
        if high != low and high < count:
            route += [(low, high), (high, low)]
    return lax.ppermute(block, axis, route)


def padded_2(cells, sides, width):
    for axis, dim in sides:
        count = lax.axis_size(axis)
        head = lax.slice_in_dim(cells, 0, width, axis=dim)
        tail = lax.slice_in_dim(cells, cells.shape[dim] - width, cells.shape[dim], axis=dim)
        cells = jnp.concatenate(
            [
                lax.ppermute(tail, axis, [(i, (i + 1) % count) for i in range(count)]),
                cells,
                lax.ppermute(head, axis, [((i + 1) % count, i) for i in range(count)]),
            ],
            axis=dim,
        )
    return cells


def thermo(area, volume, air, temp_blocks, salt_blocks, ocean):
    freeze = -0.054 * salt_blocks
    excess = temp_blocks - freeze
    growth = KAPPA * area * (freeze - air)[:, None, :] / (volume + 0.1)
    vol_new = (volume + growth) * jnp.exp(-MELT * excess)[:, None, :]
    area_new = area * jnp.exp(-0.5 * MELT * excess)[:, None, :]
    keep = ocean[:, None, None]
    area_keep = jnp.where(keep, area_new, area)
    volume_keep = jnp.where(keep, vol_new, volume)
    conc_sum = jnp.sum(area_new, axis=1)
    mass_sum = jnp.sum(vol_new, axis=1)
    conc = jnp.where(ocean[:, None], conc_sum, jnp.zeros_like(conc_sum))
    mass = jnp.where(ocean[:, None], mass_sum, jnp.zeros_like(mass_sum))
    strength = PSTAR * mass * jnp.exp(-CSTAR * (1.0 - conc))
    return (area_keep, volume_keep, jnp.stack([mass, strength], axis=1))


def fold_partner(rows):
    partner = rows
    for bit_index in range(lax.axis_size("lon").bit_length() - 1):
        partner = swapped(partner, "lon", bit_index)
    return partner


def extend(fields, signs, which):
    if which == "speed":
        padded = padded_2(fields, (("grp", 1), ("lon", 2)), 1)
    else:
        padded = padded_2(fields, (("grp", 1), ("lon", 2)), 1)
    partner = fold_partner(fields[:, -1, :])
    mirrored = signs[:, None] * partner[:, ::-1]
    band_index = lax.axis_index("grp")
    band_count = lax.axis_size("grp")
    north = jnp.where(band_index == band_count - 1, mirrored, padded[:, -1, 1:-1])
    south = jnp.where(band_index == 0, jnp.zeros_like(mirrored), padded[:, 0, 1:-1])
    return padded.at[:, -1, 1:-1].set(north).at[:, 0, 1:-1].set(south)


def across(padded):
    return (padded[1:-1, 2:] - padded[1:-1, :-2]) * 0.5


def upward(padded):
    return (padded[2:, 1:-1] - padded[:-2, 1:-1]) * 0.5


def subcycle(velocity, stress, mass, strength, wind_stress, ocean_current, extend_fn):
    speed = extend_fn(velocity, jnp.array([-1.0, -1.0], jnp.float32), "speed")
    dudx = across(speed[0])
    dudy = upward(speed[0])
    dvdx = across(speed[1])
    dvdy = upward(speed[1])
    divu = dudx + dvdy
    tension = dudx - dvdy
    shear = dudy + dvdx
    delta = jnp.sqrt(divu * divu + (tension * tension + shear * shear) / ECC2 + DMIN2)
    ratio = strength / delta
    sig_one = (stress[0] + RELAX * (ratio * divu - strength)) / (1.0 + RELAX)
    sig_two = (stress[1] + RELAX * ratio * tension / ECC2) / (1.0 + RELAX)
    sig_shear = (stress[2] + RELAX * ratio * shear / (2.0 * ECC2)) / (1.0 + RELAX)
    new_stress = jnp.stack([sig_one, sig_two, sig_shear])
    padded = extend_fn(new_stress, jnp.array([1.0, 1.0, 1.0], jnp.float32), "stress")
    normal_x = (padded[0] + padded[1]) * 0.5
    normal_y = (padded[0] - padded[1]) * 0.5
    force_x = across(normal_x) + upward(padded[2])
    force_y = across(padded[2]) + upward(normal_y)
    inertia = mass / DTE
    denom = inertia + DRAG
    u_old = velocity[0]
    v_old = velocity[1]
    u_new = (
        inertia * u_old + force_x + wind_stress[0] + DRAG * ocean_current[0] + FCOR * mass * v_old
    ) / denom
    v_new = (
        inertia * v_old + force_y + wind_stress[1] + DRAG * ocean_current[1] - FCOR * mass * u_old
    ) / denom
    return (jnp.stack([u_new, v_new]), new_stress)


def slots_from_positions(arrived_pos, block_count, slot_count):
    lon_here = lax.axis_index("lon")
    local_index = arrived_pos.astype(jnp.int32) - lon_here * block_count
    local_index = jnp.where(arrived_pos >= 0.0, local_index, block_count)
    slot_ids = jnp.arange(slot_count, dtype=jnp.int32)
    return jnp.zeros((block_count,), jnp.int32).at[local_index].set(slot_ids, mode="drop")


def shards(
    surface_temp,
    salinity,
    wind_stress,
    ocean_current,
    velocity,
    stress,
    ice_area,
    ice_volume,
    air_temp,
    ice_mask,
    curve_pos,
):
    lon_count = lax.axis_size("lon")
    tile_rows, tile_cols = surface_temp.shape
    block_count = curve_pos.shape[0]
    capacity = 2 * block_count // lon_count
    cells = BY * BX
    slot_count = lon_count * capacity

    def pack(field_grid):
        shaped = field_grid.reshape(tile_rows // BY, BY, tile_cols // BX, BX).transpose(0, 2, 1, 3)
        return shaped.reshape(block_count, cells)

    def unpack(block_rows):
        shaped = block_rows.reshape(tile_rows // BY, tile_cols // BX, BY, BX).transpose(0, 2, 1, 3)
        return shaped.reshape(tile_rows, tile_cols)

    targets = curve_pos // block_count
    indices = jnp.arange(block_count, dtype=jnp.int32)
    ranking = jnp.sum(
        ((targets[:, None] == targets[None, :]) & (indices[None, :] < indices[:, None])).astype(
            jnp.int32
        ),
        axis=1,
    )
    send_slot = targets * capacity + ranking
    ocean = ice_mask > 0
    pos_slots = (
        jnp.full((slot_count,), -1.0, jnp.float32).at[send_slot].set(curve_pos.astype(jnp.float32))
    )
    payload = jnp.stack([pack(surface_temp), pack(salinity)], axis=1)
    outgoing = jnp.zeros((slot_count, 2, cells), jnp.float32).at[send_slot].set(payload)
    incoming, in_pos = (
        lax.all_to_all(outgoing, "lon", split_axis=0, concat_axis=0, tiled=True),
        lax.all_to_all(pos_slots, "lon", split_axis=0, concat_axis=0, tiled=True),
    )
    arrive_slot = slots_from_positions(in_pos, block_count, slot_count)
    arrived = incoming[arrive_slot]
    area_out, volume_out, coupled = thermo(
        ice_area, ice_volume, air_temp, arrived[:, 0], arrived[:, 1], ocean
    )
    replies = jnp.zeros((slot_count, 2, cells), jnp.float32).at[arrive_slot].set(coupled)
    returned = lax.all_to_all(replies, "lon", split_axis=0, concat_axis=0, tiled=True)
    coupled_tile = returned[send_slot]
    mass = unpack(coupled_tile[:, 0])
    strength = unpack(coupled_tile[:, 1])
    speed_now = velocity
    stress_now = stress
    for substep in range(SUB):
        speed_now, stress_now = subcycle(
            speed_now, stress_now, mass, strength, wind_stress, ocean_current, extend
        )
    return (speed_now, stress_now, area_out, volume_out)


def solution(mesh):
    return jax.shard_map(
        shards,
        mesh=mesh,
        in_specs=(
            P("grp", "lon"),
            P("grp", "lon"),
            P(None, "grp", "lon"),
            P(None, "grp", "lon"),
            P(None, "grp", "lon"),
            P(None, "grp", "lon"),
            P(("grp", "lon"), None, None),
            P(("grp", "lon"), None, None),
            P(("grp", "lon"), None),
            P(("grp", "lon")),
            P(("grp", "lon")),
        ),
        out_specs=(
            P(None, "grp", "lon"),
            P(None, "grp", "lon"),
            P(("grp", "lon"), None, None),
            P(("grp", "lon"), None, None),
        ),
        check_vma=False,
    )
```

profile of v0, /device:TPU:6, one launch (start us, length us, event | category | flops | bytes accessed | tf_op | source)
XLA Modules:
  0.0 257.7 jit_solution(9390111333446243070)
XLA Ops:
  2.9 4.9 %all-to-all-start = ((f32[8,8,1]{1,2,0:T(1,128)}), f32[8,8,1]{1,2,0:T(1,128)S(1)}, u32[]{:S(2)}, u32[]{:S(2)}) async-start(f32[8,8,1]{1,2,0:T(1,128)} %bitcast), calls=%async_computation | async-start | bytes 8192 | tf_op jit(solution)/shard_map/all_to_all | solution.py:181
  12.2 4.4 %scatter_fusion = f32[64,2,2048]{2,1,0:T(2,128)} fusion(f32[64,2,2048]{2,1,0:T(2,128)} %broadcast.441.clone, s32[32]{0:T(128)S(1)} %compare_select_fusion.3, f32[32,2,2048]{2,1,0:T(2,128)S(1)} %pad_maximum_fusion.9), kind=kCustom, calls=%fused_computation.4 | custom fusion | bytes 1572992 | tf_op jit(solution)/shard_map/scatter | solution.py:178
  16.6 5.2 %all-to-all-start.1 = ((f32[64,2,2048]{2,1,0:T(2,128)}), f32[64,2,2048]{2,1,0:T(2,128)S(1)}, u32[]{:S(2)}, u32[]{:S(2)}) async-start(f32[64,2,2048]{2,1,0:T(2,128)} %scatter_fusion), calls=%async_computation.1 | async-start | bytes 2097152 | tf_op jit(solution)/shard_map/all_to_all | solution.py:180
  22.7 25.6 %all-to-all-done.1 = f32[64,2,2048]{2,1,0:T(2,128)S(1)} async-done(((f32[64,2,2048]{2,1,0:T(2,128)}), f32[64,2,2048]{2,1,0:T(2,128)S(1)}, u32[]{:S(2)}, u32[]{:S(2)}) %all-to-all-start.1) | async-done | bytes 1048608 | tf_op jit(solution)/shard_map/all_to_all | solution.py:180
  55.4 4.3 %scatter_fusion.1 = f32[64,2,2048]{2,1,0:T(2,128)} fusion(f32[64,2,2048]{2,1,0:T(2,128)} %broadcast.441, s32[32]{0:T(128)S(1)} %compare_select_fusion.1, f32[32,2,2048]{2,1,0:T(2,128)S(1)} %copy.232), kind=kCustom, calls=%fused_computation.5 | custom fusion | bytes 1572992 | tf_op jit(solution)/shard_map/scatter | solution.py:188
  59.7 3.7 %all-to-all-start.2 = ((f32[64,2,2048]{2,1,0:T(2,128)}), f32[64,2,2048]{2,1,0:T(2,128)S(1)}, u32[]{:S(2)}, u32[]{:S(2)}) async-start(f32[64,2,2048]{2,1,0:T(2,128)} %scatter_fusion.1), calls=%async_computation.2 | async-start | bytes 2097152 | tf_op jit(solution)/shard_map/all_to_all | solution.py:189
  68.8 2.9 %collective-permute-start.3 = (f32[2,66,1]{2,1,0:T(8,128)S(1)}, f32[2,66,1]{2,1,0:T(8,128)S(1)}, u32[]{:S(2)}, u32[]{:S(2)}) collective-permute-start(f32[2,66,1]{2,1,0:T(8,128)S(1)} %get-tuple-element.266), channel_id=1, source_target_pairs={{1,0},{2,1},{3,2},{4,3},{5,4},{6,5},{7,6},{0,7},{9,8},{10,9},{11,1... | collective-permute-start | bytes 1592 | tf_op jit(solution)/shard_map/ppermute | solution.py:42
  71.8 10.0 %collective-permute-done.5 = f32[2,1024]{1,0:T(2,128)S(1)} collective-permute-done((f32[2,1024]{1,0:T(2,128)S(1)}, f32[2,1024]{1,0:T(2,128)S(1)}, u32[]{:S(2)}, u32[]{:S(2)}) %collective-permute-start.5) | collective-permute-done | bytes 8224 | tf_op jit(solution)/shard_map/ppermute | solution.py:30
  81.8 4.7 %collective-permute-start.6 = (f32[2,1024]{1,0:T(2,128)S(1)}, f32[2,1024]{1,0:T(2,128)S(1)}, u32[]{:S(2)}, u32[]{:S(2)}) collective-permute-start(f32[2,1024]{1,0:T(2,128)S(1)} %collective-permute-done.5), channel_id=1, source_target_pairs={{0,4},{4,0},{1,5},{5,1},{2,6},{6,2},{3,7},{7,3},{8,12},{12,8},{9,1... | collective-permute-start | bytes 24584 | tf_op jit(solution)/shard_map/ppermute | solution.py:30
  86.9 5.0 %collective-permute-done.6 = f32[2,1024]{1,0:T(2,128)S(1)} collective-permute-done((f32[2,1024]{1,0:T(2,128)S(1)}, f32[2,1024]{1,0:T(2,128)S(1)}, u32[]{:S(2)}, u32[]{:S(2)}) %collective-permute-start.6) | collective-permute-done | bytes 8224 | tf_op jit(solution)/shard_map/ppermute | solution.py:30
  108.8 2.9 %collective-permute-done.9 = f32[3,66,1]{2,1,0:T(8,128)S(1)} collective-permute-done((f32[3,66,1]{2,1,0:T(8,128)S(1)}, f32[3,66,1]{2,1,0:T(8,128)S(1)}, u32[]{:S(2)}, u32[]{:S(2)}) %collective-permute-start.9) | collective-permute-done | bytes 824 | tf_op jit(solution)/shard_map/ppermute | solution.py:40
  116.1 3.3 %scatter.91 = f32[3,66,1026]{2,1,0:T(8,128)} dynamic-update-slice(f32[3,66,1026]{2,1,0:T(8,128)} %scatter.90, f32[3,1,1024]{2,1,0:T(1,128)S(1)} %broadcast_select_fusion.1, s32[]{:T(128)} %constant.430.clone.1, s32[]{:T(128)} %bitcast.17, s32[]{:T(128)} %bitcast.18) | dynamic-update-slice | bytes 24580 | tf_op jit(solution)/shard_map/scatter | solution.py:84
  132.1 2.9 %collective-permute-done.16 = f32[2,66,1]{2,1,0:T(8,128)S(1)} collective-permute-done((f32[2,66,1]{2,1,0:T(8,128)S(1)}, f32[2,66,1]{2,1,0:T(8,128)S(1)}, u32[]{:S(2)}, u32[]{:S(2)}) %collective-permute-start.16) | collective-permute-done | bytes 560 | tf_op jit(solution)/shard_map/ppermute | solution.py:40
  139.8 3.1 %scatter.95 = f32[2,66,1026]{2,1,0:T(8,128)} dynamic-update-slice(f32[2,66,1026]{2,1,0:T(8,128)} %scatter.94, f32[2,1,1024]{2,1,0:T(1,128)S(1)} %copy.248, s32[]{:T(128)} %constant.430.clone.1, s32[]{:T(128)} %bitcast.17, s32[]{:T(128)} %bitcast.18) | dynamic-update-slice | bytes 16388 | tf_op jit(solution)/shard_map/scatter | solution.py:84
  151.1 3.2 %collective-permute-done.26 = f32[3,1024]{1,0:T(4,128)} collective-permute-done((f32[3,1024]{1,0:T(4,128)S(1)}, f32[3,1024]{1,0:T(4,128)}, u32[]{:S(2)}, u32[]{:S(2)}) %collective-permute-start.26) | collective-permute-done | bytes 12320 | tf_op jit(solution)/shard_map/ppermute | solution.py:30
  162.0 3.3 %scatter.99 = f32[3,66,1026]{2,1,0:T(8,128)} dynamic-update-slice(f32[3,66,1026]{2,1,0:T(8,128)} %scatter.96, f32[3,1,1024]{2,1,0:T(1,128)S(1)} %copy.254, s32[]{:T(128)} %constant.430.clone.1, s32[]{:T(128)} %bitcast.17, s32[]{:T(128)} %bitcast.18) | dynamic-update-slice | bytes 24580 | tf_op jit(solution)/shard_map/scatter | solution.py:84
  167.3 2.8 %collective-permute-start.29 = (f32[2,1,1024]{2,0,1:T(2,128)S(1)}, f32[2,1,1024]{2,0,1:T(2,128)S(1)}, u32[]{:S(2)}, u32[]{:S(2)}) collective-permute-start(f32[2,1,1024]{2,0,1:T(2,128)S(1)} %copy.287), channel_id=1, source_target_pairs={{8,0},{16,8},{24,16},{0,24},{9,1},{17,9},{25,17},{1,25},{10,2},{18... | collective-permute-start | bytes 24584 | tf_op jit(solution)/shard_map/ppermute | solution.py:42
  174.7 2.8 %collective-permute-done.33 = f32[2,1024]{1,0:T(2,128)S(1)} collective-permute-done((f32[2,1024]{1,0:T(2,128)S(1)}, f32[2,1024]{1,0:T(2,128)S(1)}, u32[]{:S(2)}, u32[]{:S(2)}) %collective-permute-start.33) | collective-permute-done | bytes 8224 | tf_op jit(solution)/shard_map/ppermute | solution.py:30
  184.7 3.1 %scatter.121 = f32[2,66,1026]{2,1,0:T(8,128)} dynamic-update-slice(f32[2,66,1026]{2,1,0:T(8,128)} %scatter.120, f32[2,1,1024]{2,1,0:T(1,128)S(1)} %copy.260, s32[]{:T(128)} %constant.430.clone.1, s32[]{:T(128)} %bitcast.17, s32[]{:T(128)} %bitcast.18) | dynamic-update-slice | bytes 16388 | tf_op jit(solution)/shard_map/scatter | solution.py:84
  207.8 3.3 %scatter.123 = f32[3,66,1026]{2,1,0:T(8,128)} dynamic-update-slice(f32[3,66,1026]{2,1,0:T(8,128)} %scatter.122, f32[3,1,1024]{2,1,0:T(1,128)S(1)} %copy.266, s32[]{:T(128)} %constant.430.clone.1, s32[]{:T(128)} %bitcast.17, s32[]{:T(128)} %bitcast.18) | dynamic-update-slice | bytes 24580 | tf_op jit(solution)/shard_map/scatter | solution.py:84
  221.5 3.1 %collective-permute-done.44 = f32[2,66,1]{2,0,1:T(2,128)S(1)} collective-permute-done((f32[2,66,1]{2,0,1:T(2,128)S(1)}, f32[2,66,1]{2,0,1:T(2,128)S(1)}, u32[]{:S(2)}, u32[]{:S(2)}) %collective-permute-start.44) | collective-permute-done | bytes 560 | tf_op jit(solution)/shard_map/ppermute | solution.py:40
  229.1 2.7 %scatter.125 = f32[2,66,1026]{2,0,1:T(2,128)} dynamic-update-slice(f32[2,66,1026]{2,0,1:T(2,128)} %scatter.124, f32[2,1,1024]{2,0,1:T(2,128)S(1)} %broadcast_select_fusion.8, s32[]{:T(128)} %constant.430.clone.1, s32[]{:T(128)} %bitcast.17, s32[]{:T(128)} %bitcast.18) | dynamic-update-slice | bytes 16388 | tf_op jit(solution)/shard_map/scatter | solution.py:84
  241.1 3.1 %collective-permute-done.54 = f32[3,1024]{1,0:T(4,128)S(1)} collective-permute-done((f32[3,1024]{1,0:T(4,128)S(1)}, f32[3,1024]{1,0:T(4,128)S(1)}, u32[]{:S(2)}, u32[]{:S(2)}) %collective-permute-start.54) | collective-permute-done | bytes 12320 | tf_op jit(solution)/shard_map/ppermute | solution.py:30
  251.7 3.3 %scatter.127 = f32[3,66,1026]{2,1,0:T(8,128)} dynamic-update-slice(f32[3,66,1026]{2,1,0:T(8,128)} %scatter.126, f32[3,1,1024]{2,1,0:T(1,128)S(1)} %copy.273, s32[]{:T(128)} %constant.430.clone.1, s32[]{:T(128)} %bitcast.17, s32[]{:T(128)} %bitcast.18) | dynamic-update-slice | bytes 24580 | tf_op jit(solution)/shard_map/scatter | solution.py:84
  (328 shorter events, 142.1 us)
Async XLA Ops:
  2.9 13.6 %all-to-all-start = ((f32[8,8,1]{1,2,0:T(1,128)}), f32[8,8,1]{1,2,0:T(1,128)S(1)}, u32[]{:S(2)}, u32[]{:S(2)}) async-start(f32[8,8,1]{1,2,0:T(1,128)} %bitcast), calls=%async_computation | async-start | bytes 8192 | tf_op jit(solution)/shard_map/all_to_all | solution.py:181
  16.6 31.8 %all-to-all-start.1 = ((f32[64,2,2048]{2,1,0:T(2,128)}), f32[64,2,2048]{2,1,0:T(2,128)S(1)}, u32[]{:S(2)}, u32[]{:S(2)}) async-start(f32[64,2,2048]{2,1,0:T(2,128)} %scatter_fusion), calls=%async_computation.1 | async-start | bytes 2097152 | tf_op jit(solution)/shard_map/all_to_all | solution.py:180
  59.7 35.6 %all-to-all-start.2 = ((f32[64,2,2048]{2,1,0:T(2,128)}), f32[64,2,2048]{2,1,0:T(2,128)S(1)}, u32[]{:S(2)}, u32[]{:S(2)}) async-start(f32[64,2,2048]{2,1,0:T(2,128)} %scatter_fusion.1), calls=%async_computation.2 | async-start | bytes 2097152 | tf_op jit(solution)/shard_map/all_to_all | solution.py:189
  63.4 5.2 %collective-permute-start = (f32[2,1,1024]{2,1,0:T(1,128)S(1)}, f32[2,1,1024]{2,1,0:T(1,128)S(1)}, u32[]{:S(2)}, u32[]{:S(2)}) collective-permute-start(f32[2,1,1024]{2,1,0:T(1,128)S(1)} %get-tuple-element.276), channel_id=1, source_target_pairs={{0,8},{8,16},{16,24},{24,0},{1,9},{9,17},{17,25},{25,1},{2,10},{10... | collective-permute-start | bytes 24584 | tf_op jit(solution)/shard_map/ppermute | solution.py:40
  66.3 15.5 %collective-permute-start.5 = (f32[2,1024]{1,0:T(2,128)S(1)}, f32[2,1024]{1,0:T(2,128)S(1)}, u32[]{:S(2)}, u32[]{:S(2)}) collective-permute-start(f32[2,1024]{1,0:T(2,128)S(1)} %collective-permute-done.4), channel_id=1, source_target_pairs={{0,2},{2,0},{1,3},{3,1},{4,6},{6,4},{5,7},{7,5},{8,10},{10,8},{9,1... | collective-permute-start | bytes 24584 | tf_op jit(solution)/shard_map/ppermute | solution.py:30
  68.8 17.7 %collective-permute-start.3 = (f32[2,66,1]{2,1,0:T(8,128)S(1)}, f32[2,66,1]{2,1,0:T(8,128)S(1)}, u32[]{:S(2)}, u32[]{:S(2)}) collective-permute-start(f32[2,66,1]{2,1,0:T(8,128)S(1)} %get-tuple-element.266), channel_id=1, source_target_pairs={{1,0},{2,1},{3,2},{4,3},{5,4},{6,5},{7,6},{0,7},{9,8},{10,9},{11,1... | collective-permute-start | bytes 1592 | tf_op jit(solution)/shard_map/ppermute | solution.py:42
  71.8 14.8 %collective-permute-start.2 = (f32[2,66,1]{2,1,0:T(8,128)S(1)}, f32[2,66,1]{2,1,0:T(8,128)S(1)}, u32[]{:S(2)}, u32[]{:S(2)}) collective-permute-start(f32[2,66,1]{2,1,0:T(8,128)S(1)} %get-tuple-element.267), channel_id=1, source_target_pairs={{0,1},{1,2},{2,3},{3,4},{4,5},{5,6},{6,7},{7,0},{8,9},{9,10},{10,1... | collective-permute-start | bytes 1592 | tf_op jit(solution)/shard_map/ppermute | solution.py:40
  81.8 10.1 %collective-permute-start.6 = (f32[2,1024]{1,0:T(2,128)S(1)}, f32[2,1024]{1,0:T(2,128)S(1)}, u32[]{:S(2)}, u32[]{:S(2)}) collective-permute-start(f32[2,1024]{1,0:T(2,128)S(1)} %collective-permute-done.5), channel_id=1, source_target_pairs={{0,4},{4,0},{1,5},{5,1},{2,6},{6,2},{3,7},{7,3},{8,12},{12,8},{9,1... | collective-permute-start | bytes 24584 | tf_op jit(solution)/shard_map/ppermute | solution.py:30
  100.6 4.7 %collective-permute-start.8 = (f32[3,1,1024]{2,0,1:T(4,128)S(1)}, f32[3,1,1024]{2,0,1:T(4,128)S(1)}, u32[]{:S(2)}, u32[]{:S(2)}) collective-permute-start(f32[3,1,1024]{2,0,1:T(4,128)S(1)} %copy.281), channel_id=1, source_target_pairs={{8,0},{16,8},{24,16},{0,24},{9,1},{17,9},{25,17},{1,25},{10,2},{18... | collective-permute-start | bytes 36872 | tf_op jit(solution)/shard_map/ppermute | solution.py:42
  105.6 6.0 %collective-permute-start.9 = (f32[3,66,1]{2,1,0:T(8,128)S(1)}, f32[3,66,1]{2,1,0:T(8,128)S(1)}, u32[]{:S(2)}, u32[]{:S(2)}) collective-permute-start(f32[3,66,1]{2,1,0:T(8,128)S(1)} %get-tuple-element.245), channel_id=1, source_target_pairs={{0,1},{1,2},{2,3},{3,4},{4,5},{5,6},{6,7},{7,0},{8,9},{9,10},{10,1... | collective-permute-start | bytes 2384 | tf_op jit(solution)/shard_map/ppermute | solution.py:40
  107.6 5.6 %collective-permute-start.13 = (f32[3,1024]{1,0:T(4,128)S(1)}, f32[3,1024]{1,0:T(4,128)S(1)}, u32[]{:S(2)}, u32[]{:S(2)}) collective-permute-start(f32[3,1024]{1,0:T(4,128)S(1)} %collective-permute-done.12), channel_id=1, source_target_pairs={{0,4},{4,0},{1,5},{5,1},{2,6},{6,2},{3,7},{7,3},{8,12},{12,8},{9,1... | collective-permute-start | bytes 36872 | tf_op jit(solution)/shard_map/ppermute | solution.py:30
  122.3 4.8 %collective-permute-start.15 = (f32[2,1,1024]{2,0,1:T(2,128)S(1)}, f32[2,1,1024]{2,0,1:T(2,128)S(1)}, u32[]{:S(2)}, u32[]{:S(2)}) collective-permute-start(f32[2,1,1024]{2,0,1:T(2,128)S(1)} %copy.283), channel_id=1, source_target_pairs={{8,0},{16,8},{24,16},{0,24},{9,1},{17,9},{25,17},{1,25},{10,2},{18... | collective-permute-start | bytes 24584 | tf_op jit(solution)/shard_map/ppermute | solution.py:42
  129.3 5.7 %collective-permute-start.16 = (f32[2,66,1]{2,1,0:T(8,128)S(1)}, f32[2,66,1]{2,1,0:T(8,128)S(1)}, u32[]{:S(2)}, u32[]{:S(2)}) collective-permute-start(f32[2,66,1]{2,1,0:T(8,128)S(1)} %get-tuple-element.265), channel_id=1, source_target_pairs={{0,1},{1,2},{2,3},{3,4},{4,5},{5,6},{6,7},{7,0},{8,9},{9,10},{10,1... | collective-permute-start | bytes 1592 | tf_op jit(solution)/shard_map/ppermute | solution.py:40
  132.0 5.1 %collective-permute-start.20 = (f32[2,1024]{1,0:T(2,128)S(1)}, f32[2,1024]{1,0:T(2,128)S(1)}, u32[]{:S(2)}, u32[]{:S(2)}) collective-permute-start(f32[2,1024]{1,0:T(2,128)S(1)} %collective-permute-done.19), channel_id=1, source_target_pairs={{0,4},{4,0},{1,5},{5,1},{2,6},{6,2},{3,7},{7,3},{8,12},{12,8},{9,1... | collective-permute-start | bytes 24584 | tf_op jit(solution)/shard_map/ppermute | solution.py:30
  145.3 4.7 %collective-permute-start.22 = (f32[3,1,1024]{2,0,1:T(4,128)S(1)}, f32[3,1,1024]{2,0,1:T(4,128)S(1)}, u32[]{:S(2)}, u32[]{:S(2)}) collective-permute-start(f32[3,1,1024]{2,0,1:T(4,128)S(1)} %copy.285), channel_id=1, source_target_pairs={{8,0},{16,8},{24,16},{0,24},{9,1},{17,9},{25,17},{1,25},{10,2},{18... | collective-permute-start | bytes 36872 | tf_op jit(solution)/shard_map/ppermute | solution.py:42
  150.7 6.4 %collective-permute-start.23 = (f32[3,66,1]{2,1,0:T(8,128)S(1)}, f32[3,66,1]{2,1,0:T(8,128)}, u32[]{:S(2)}, u32[]{:S(2)}) collective-permute-start(f32[3,66,1]{2,1,0:T(8,128)S(1)} %get-tuple-element.243), channel_id=1, source_target_pairs={{0,1},{1,2},{2,3},{3,4},{4,5},{5,6},{6,7},{7,0},{8,9},{9,10},{10,1... | collective-permute-start | bytes 2384 | tf_op jit(solution)/shard_map/ppermute | solution.py:40
  154.3 4.8 %collective-permute-start.27 = (f32[3,1024]{1,0:T(4,128)}, f32[3,1024]{1,0:T(4,128)S(1)}, u32[]{:S(2)}, u32[]{:S(2)}) collective-permute-start(f32[3,1024]{1,0:T(4,128)} %collective-permute-done.26), channel_id=1, source_target_pairs={{0,4},{4,0},{1,5},{5,1},{2,6},{6,2},{3,7},{7,3},{8,12},{12,8},{9,1... | collective-permute-start | bytes 36872 | tf_op jit(solution)/shard_map/ppermute | solution.py:30
  174.2 5.6 %collective-permute-start.30 = (f32[2,66,1]{2,1,0:T(8,128)S(1)}, f32[2,66,1]{2,1,0:T(8,128)S(1)}, u32[]{:S(2)}, u32[]{:S(2)}) collective-permute-start(f32[2,66,1]{2,1,0:T(8,128)S(1)} %get-tuple-element.263), channel_id=1, source_target_pairs={{0,1},{1,2},{2,3},{3,4},{4,5},{5,6},{6,7},{7,0},{8,9},{9,10},{10,1... | collective-permute-start | bytes 1592 | tf_op jit(solution)/shard_map/ppermute | solution.py:40
  190.4 4.7 %collective-permute-start.36 = (f32[3,1,1024]{2,0,1:T(4,128)S(1)}, f32[3,1,1024]{2,0,1:T(4,128)S(1)}, u32[]{:S(2)}, u32[]{:S(2)}) collective-permute-start(f32[3,1,1024]{2,0,1:T(4,128)S(1)} %copy.289), channel_id=1, source_target_pairs={{8,0},{16,8},{24,16},{0,24},{9,1},{17,9},{25,17},{1,25},{10,2},{18... | collective-permute-start | bytes 36872 | tf_op jit(solution)/shard_map/ppermute | solution.py:42
  196.6 6.2 %collective-permute-start.37 = (f32[3,66,1]{2,1,0:T(8,128)S(1)}, f32[3,66,1]{2,1,0:T(8,128)}, u32[]{:S(2)}, u32[]{:S(2)}) collective-permute-start(f32[3,66,1]{2,1,0:T(8,128)S(1)} %get-tuple-element.241), channel_id=1, source_target_pairs={{0,1},{1,2},{2,3},{3,4},{4,5},{5,6},{6,7},{7,0},{8,9},{9,10},{10,1... | collective-permute-start | bytes 2384 | tf_op jit(solution)/shard_map/ppermute | solution.py:40
  199.3 5.6 %collective-permute-start.41 = (f32[3,1024]{1,0:T(4,128)}, f32[3,1024]{1,0:T(4,128)S(1)}, u32[]{:S(2)}, u32[]{:S(2)}) collective-permute-start(f32[3,1024]{1,0:T(4,128)} %collective-permute-done.40), channel_id=1, source_target_pairs={{0,4},{4,0},{1,5},{5,1},{2,6},{6,2},{3,7},{7,3},{8,12},{12,8},{9,1... | collective-permute-start | bytes 36872 | tf_op jit(solution)/shard_map/ppermute | solution.py:30
  219.0 5.6 %collective-permute-start.44 = (f32[2,66,1]{2,0,1:T(2,128)S(1)}, f32[2,66,1]{2,0,1:T(2,128)S(1)}, u32[]{:S(2)}, u32[]{:S(2)}) collective-permute-start(f32[2,66,1]{2,0,1:T(2,128)S(1)} %get-tuple-element.269), channel_id=1, source_target_pairs={{0,1},{1,2},{2,3},{3,4},{4,5},{5,6},{6,7},{7,0},{8,9},{9,10},{10,1... | collective-permute-start | bytes 1592 | tf_op jit(solution)/shard_map/ppermute | solution.py:40
  220.1 6.8 %collective-permute-start.48 = (f32[2,1024]{1,0:T(2,128)S(1)}, f32[2,1024]{1,0:T(2,128)S(1)}, u32[]{:S(2)}, u32[]{:S(2)}) collective-permute-start(f32[2,1024]{1,0:T(2,128)S(1)} %collective-permute-done.47), channel_id=1, source_target_pairs={{0,4},{4,0},{1,5},{5,1},{2,6},{6,2},{3,7},{7,3},{8,12},{12,8},{9,1... | collective-permute-start | bytes 24584 | tf_op jit(solution)/shard_map/ppermute | solution.py:30
  240.6 6.1 %collective-permute-start.51 = (f32[3,66,1]{2,1,0:T(8,128)S(1)}, f32[3,66,1]{2,1,0:T(8,128)S(1)}, u32[]{:S(2)}, u32[]{:S(2)}) collective-permute-start(f32[3,66,1]{2,1,0:T(8,128)S(1)} %get-tuple-element.239), channel_id=1, source_target_pairs={{0,1},{1,2},{2,3},{3,4},{4,5},{5,6},{6,7},{7,0},{8,9},{9,10},{10,1... | collective-permute-start | bytes 2384 | tf_op jit(solution)/shard_map/ppermute | solution.py:40
  (66 other events, 295.5 us)
where the time goes:
time: 262 us; the launch traced here: 258 us
  waiting for transfers between devices  91.1 us (35%)
  local copies, waits for them, and re-layouts  87.7 us (33%)
  starting transfers between devices  55.3 us (21%)
  other arithmetic  21.8 us (8%)
    scatter x16, local copies, waits for them, and re-layouts, extend(): return padded.at[:, -1, 1:-1].set(north).at[:, 0, 1:-1].set(south)  38.7 us
    ppermute x24, waiting for transfers between devices, swapped(): return lax.ppermute(block, axis, route)  31.8 us
    all_to_all x1, waiting for transfers between devices, shards(): lax.all_to_all(outgoing, 'lon', split_axis=0, concat_axis=0, tiled=True)  25.6 us
    ppermute x16, waiting for transfers between devices, padded_2(): lax.ppermute(tail, axis, [(i, (i + 1) % count) for i in range(count)])  20.9 us
    ppermute x16, starting transfers between devices, padded_2(): lax.ppermute(head, axis, [((i + 1) % count, i) for i in range(count)])  16.4 us
    concatenate x8, local copies, waits for them, and re-layouts, padded_2(): jnp.concatenate([lax.ppermute(tail, axis, [(i, (i + 1) % count) for i in...  14.2 us
    ppermute x16, starting transfers between devices, padded_2(): lax.ppermute(tail, axis, [(i, (i + 1) % count) for i in range(count)])  13.9 us
    ppermute x16, waiting for transfers between devices, padded_2(): lax.ppermute(head, axis, [((i + 1) % count, i) for i in range(count)])  12.8 us
  transfers between devices with their start and end apart: 59, of which 35 were waited for; matrix products, arithmetic and copies ran while one was open for 12% of the time, Pallas kernels for 0%

commit v1 on v0

v1 whole, which is shorter than its diff:
```python
import functools

import jax
import jax.numpy as jnp
from jax import lax
from jax.experimental import pallas as pl
from jax.experimental.pallas import tpu as pltpu
from jax.sharding import PartitionSpec as P

BY = 8
BX = 256
SUB = 4

KAPPA = 0.02
MELT = 0.6
PSTAR = 10.0
CSTAR = 20.0
RELAX = 0.4
FCOR = 0.3

HALO = 2 * SUB
PAD = 8
LANES = 128
MESH = pl.DeviceIdType.MESH

N_FIELD = 9


def thermo(area, volume, air, temp_blocks, salt_blocks, ocean):
    freeze = -0.054 * salt_blocks
    excess = temp_blocks - freeze
    growth = KAPPA * area * (freeze - air)[:, None, :] / (volume + 0.1)
    vol_new = (volume + growth) * jnp.exp(-MELT * excess)[:, None, :]
    area_new = area * jnp.exp(-0.5 * MELT * excess)[:, None, :]
    keep = ocean[:, None, None]
    area_keep = jnp.where(keep, area_new, area)
    volume_keep = jnp.where(keep, vol_new, volume)
    conc_sum = jnp.sum(area_new, axis=1)
    mass_sum = jnp.sum(vol_new, axis=1)
    conc = jnp.where(ocean[:, None], conc_sum, jnp.zeros_like(conc_sum))
    mass = jnp.where(ocean[:, None], mass_sum, jnp.zeros_like(mass_sum))
    strength = PSTAR * mass * jnp.exp(-CSTAR * (1.0 - conc))
    return (area_keep, volume_keep, jnp.stack([mass, strength], axis=1))


def dynamics_kernel(
    n_grp, n_lon, vel_ref, str_ref, wind_ref, cur_ref, mass_ref, stg_ref, vel_out, str_out,
    ext, inv, mir, out_e, out_w, in_w, in_e, row_send, row_recv, col_send, col_recv,
):
    rows, cols = mass_ref.shape
    wide = cols + LANES
    top = PAD + HALO
    tall = rows + 2 * HALO
    g = lax.axis_index("grp")
    l = lax.axis_index("lon")
    east = lax.rem(l + 1, n_lon)
    west = lax.rem(l + n_lon - 1, n_lon)
    mirror = n_lon - 1 - l
    not_south = g > 0
    not_north = g < n_grp - 1
    north_g = jnp.where(not_north, g + 1, g)
    north_l = jnp.where(not_north, l, mirror)

    barrier = pltpu.get_barrier_semaphore()
    pl.semaphore_signal(barrier, inc=1, device_id={"grp": g, "lon": east}, device_id_type=MESH)
    pl.semaphore_signal(barrier, inc=1, device_id={"grp": g, "lon": west}, device_id_type=MESH)
    pl.semaphore_signal(
        barrier, inc=1, device_id={"grp": north_g, "lon": north_l}, device_id_type=MESH
    )

    @pl.when(not_south)
    def _():
        pl.semaphore_signal(
            barrier, inc=1, device_id={"grp": g - 1, "lon": l}, device_id_type=MESH
        )

    body = pl.ds(top, rows)
    main = pl.ds(0, cols)
    for f in range(2):
        ext[f, body, main] = vel_ref[f]
        ext[5 + f, body, main] = wind_ref[f] + cur_ref[f]
    for f in range(3):
        ext[2 + f, body, main] = str_ref[f]
    ext[7, body, main] = mass_ref[...]
    ext[8, body, main] = stg_ref[...]
    for f in range(N_FIELD):
        ext[f, pl.ds(0, PAD), :] = jnp.zeros((PAD, wide), jnp.float32)
        ext[f, pl.ds(top + rows + HALO, PAD), :] = jnp.zeros((PAD, wide), jnp.float32)

    @pl.when(jnp.logical_not(not_south))
    def _():
        for f in range(N_FIELD):
            ext[f, pl.ds(PAD, HALO), main] = jnp.zeros((HALO, cols), jnp.float32)

    @pl.when(jnp.logical_not(not_north))
    def _():
        a = lax.broadcasted_iota(jnp.int32, (LANES, LANES), 0)
        b = lax.broadcasted_iota(jnp.int32, (LANES, LANES), 1)
        flip = (a + b == LANES - 1).astype(jnp.float32)
        for f in range(N_FIELD):
            sign = -1.0 if f in (0, 1, 5, 6) else 1.0
            for c in range(cols // LANES):
                x = ext[f, pl.ds(top + rows - HALO, HALO), pl.ds(c * LANES, LANES)]
                y = sign * jnp.dot(
                    x, flip, precision=lax.Precision.HIGHEST, preferred_element_type=jnp.float32
                )
                for r in range(HALO):
                    mir[f, pl.ds(HALO - 1 - r, 1), pl.ds(cols - (c + 1) * LANES, LANES)] = y[
                        r : r + 1
                    ]

    pl.semaphore_wait(barrier, jnp.where(not_south, 4, 3))

    low = ext.at[:, pl.ds(PAD, HALO), main]
    high = ext.at[:, pl.ds(top + rows, HALO), main]
    first = ext.at[:, pl.ds(top, HALO), main]
    last = ext.at[:, pl.ds(top + rows - HALO, HALO), main]
    to_south = pltpu.make_async_remote_copy(
        src_ref=first, dst_ref=high, send_sem=row_send.at[0], recv_sem=row_recv.at[0],
        device_id={"grp": jnp.where(not_south, g - 1, g), "lon": l}, device_id_type=MESH,
    )
    to_north = pltpu.make_async_remote_copy(
        src_ref=last, dst_ref=low, send_sem=row_send.at[1], recv_sem=row_recv.at[1],
        device_id={"grp": north_g, "lon": l}, device_id_type=MESH,
    )
    to_mirror = pltpu.make_async_remote_copy(
        src_ref=mir, dst_ref=high, send_sem=row_send.at[1], recv_sem=row_recv.at[0],
        device_id={"grp": g, "lon": mirror}, device_id_type=MESH,
    )

    @pl.when(not_south)
    def _():
        to_south.start()

    @pl.when(not_north)
    def _():
        to_north.start()

    @pl.when(jnp.logical_not(not_north))
    def _():
        to_mirror.start()

    to_south.wait_recv()

    @pl.when(not_south)
    def _():
        to_north.wait_recv()

    lane = lax.broadcasted_iota(jnp.int32, (tall, LANES), 1)
    span = pl.ds(PAD, tall)
    east_pack = jnp.zeros((tall, LANES), jnp.float32)
    west_pack = jnp.zeros((tall, LANES), jnp.float32)
    for f in range(N_FIELD):
        here = (lane >= f * HALO) & (lane < (f + 1) * HALO)
        tail = ext[f, span, pl.ds(cols - LANES, LANES)]
        head = ext[f, span, pl.ds(0, LANES)]
        east_pack = jnp.where(here, pltpu.roll(tail, ((f + 1) * HALO) % LANES, 1), east_pack)
        west_pack = jnp.where(here, pltpu.roll(head, f * HALO, 1) if f else head, west_pack)
    out_e[...] = east_pack
    out_w[...] = west_pack
    to_east = pltpu.make_async_remote_copy(
        src_ref=out_e, dst_ref=in_w, send_sem=col_send.at[0], recv_sem=col_recv.at[0],
        device_id={"grp": g, "lon": east}, device_id_type=MESH,
    )
    to_west = pltpu.make_async_remote_copy(
        src_ref=out_w, dst_ref=in_e, send_sem=col_send.at[1], recv_sem=col_recv.at[1],
        device_id={"grp": g, "lon": west}, device_id_type=MESH,
    )
    to_east.start()
    to_west.start()
    to_east.wait_recv()
    to_west.wait_recv()
    from_west = in_w[...]
    from_east = in_e[...]
    for f in range(N_FIELD):
        e = pltpu.roll(from_east, LANES - f * HALO, 1) if f else from_east
        w = pltpu.roll(from_west, LANES - (f + 1) * HALO, 1)
        ext[f, span, pl.ds(cols, LANES)] = jnp.where(
            lane < HALO, e, jnp.where(lane >= LANES - HALO, w, 0.0)
        )

    inv[...] = 1.0 / (2.0 * ext[7, span, :] + 1.0)

    @pl.when(jnp.logical_not(not_south))
    def _():
        inv[pl.ds(0, HALO), :] = jnp.zeros((HALO, wide), jnp.float32)

    @pl.when(not_south)
    def _():
        to_south.wait_send()

    @pl.when(not_north)
    def _():
        to_north.wait_send()

    @pl.when(jnp.logical_not(not_north))
    def _():
        to_mirror.wait_send()

    to_east.wait_send()
    to_west.wait_send()

    def across(x):
        return pltpu.roll(x, wide - 1, 1) - pltpu.roll(x, 1, 1)

    sub = lax.broadcasted_iota(jnp.int32, (8, wide), 0)
    is_first = sub == 0
    is_last = sub == 7

    def three(f, r):
        return (
            ext[f, pl.ds(pl.multiple_of(r - 8, 8), 8), :],
            ext[f, pl.ds(r, 8), :],
            ext[f, pl.ds(pl.multiple_of(r + 8, 8), 8), :],
        )

    def upward(strips):
        below, here, above = strips
        return pltpu.roll(jnp.where(is_first, above, here), 7, 0) - pltpu.roll(
            jnp.where(is_last, below, here), 1, 0
        )

    scale = 1.0 / (1.0 + RELAX)

    def stress_strip(i, carry):
        r = pl.multiple_of(PAD + i * 8, 8)
        at = pl.ds(r, 8)
        u = three(0, r)
        v = three(1, r)
        u_y, v_y, u_x, v_x = upward(u), upward(v), across(u[1]), across(v[1])
        divu = (u_x + v_y) * 0.5
        tension = (u_x - v_y) * 0.5
        shear = (u_y + v_x) * 0.5
        square = divu * divu + (tension * tension + shear * shear) * 0.25 + 0.01
        strength = ext[8, at, :]
        ratio = strength * lax.rsqrt(square)
        ext[2, at, :] = (ext[2, at, :] + RELAX * (ratio * divu - strength)) * scale
        ratio = ratio * scale
        ext[3, at, :] = ext[3, at, :] * scale + (RELAX / 4.0) * (ratio * tension)
        ext[4, at, :] = ext[4, at, :] * scale + (RELAX / 8.0) * (ratio * shear)
        return carry

    def speed_strip(i, carry):
        r = pl.multiple_of(PAD + i * 8, 8)
        at = pl.ds(r, 8)
        one = three(2, r)
        two = three(3, r)
        mixed = three(4, r)
        s_x = across(one[1] + two[1])
        s_y = upward([x - y for x, y in zip(one, two)])
        c_x = across(mixed[1])
        c_y = upward(mixed)
        force_x = s_x * 0.25 + c_y * 0.5
        force_y = c_x * 0.5 + s_y * 0.25
        mass = ext[7, at, :]
        factor = inv[pl.ds(pl.multiple_of(i * 8, 8), 8), :]
        u = ext[0, at, :]
        v = ext[1, at, :]
        turn = FCOR * mass
        inertia = 2.0 * mass
        ext[0, at, :] = (inertia * u + force_x + ext[5, at, :] + turn * v) * factor
        ext[1, at, :] = (inertia * v + force_y + ext[6, at, :] - turn * u) * factor
        return carry

    def step(k, carry):
        lax.fori_loop(0, tall // 8, stress_strip, 0)
        lax.fori_loop(0, tall // 8, speed_strip, 0)
        return carry

    lax.fori_loop(0, SUB, step, 0)

    for f in range(2):
        vel_out[f] = ext[f, body, main]
    for f in range(3):
        str_out[f] = ext[2 + f, body, main]


def dynamics(velocity, stress, wind_stress, ocean_current, mass, strength):
    n_grp = lax.axis_size("grp")
    n_lon = lax.axis_size("lon")
    rows, cols = mass.shape
    wide = cols + LANES
    tall = rows + 2 * HALO
    edge = pltpu.VMEM((tall, LANES), jnp.float32)
    vmem = pl.BlockSpec(memory_space=pltpu.VMEM)
    return pl.pallas_call(
        functools.partial(dynamics_kernel, n_grp, n_lon),
        out_shape=(
            jax.ShapeDtypeStruct(velocity.shape, jnp.float32),
            jax.ShapeDtypeStruct(stress.shape, jnp.float32),
        ),
        in_specs=[vmem] * 6,
        out_specs=(vmem, vmem),
        scratch_shapes=[
            pltpu.VMEM((N_FIELD, tall + 2 * PAD, wide), jnp.float32),
            pltpu.VMEM((tall, wide), jnp.float32),
            pltpu.VMEM((N_FIELD, HALO, cols), jnp.float32),
            edge, edge, edge, edge,
            pltpu.SemaphoreType.DMA((2,)),
            pltpu.SemaphoreType.DMA((2,)),
            pltpu.SemaphoreType.DMA((2,)),
            pltpu.SemaphoreType.DMA((2,)),
        ],
        compiler_params=pltpu.CompilerParams(
            collective_id=1, has_side_effects=True, vmem_limit_bytes=32 << 20
        ),
        name="dynamics",
    )(velocity, stress, wind_stress, ocean_current, mass, strength)


def shards(
    surface_temp, salinity, wind_stress, ocean_current, velocity, stress,
    ice_area, ice_volume, air_temp, ice_mask, curve_pos,
):
    lon_count = lax.axis_size("lon")
    tile_rows, tile_cols = surface_temp.shape
    block_count = curve_pos.shape[0]
    capacity = 2 * block_count // lon_count
    cells = BY * BX
    slot_count = lon_count * capacity

    def pack(field_grid):
        shaped = field_grid.reshape(tile_rows // BY, BY, tile_cols // BX, BX).transpose(0, 2, 1, 3)
        return shaped.reshape(block_count, cells)

    def unpack(block_rows):
        shaped = block_rows.reshape(tile_rows // BY, tile_cols // BX, BY, BX).transpose(0, 2, 1, 3)
        return shaped.reshape(tile_rows, tile_cols)

    targets = curve_pos // block_count
    indices = jnp.arange(block_count, dtype=jnp.int32)
    ranking = jnp.sum(
        ((targets[:, None] == targets[None, :]) & (indices[None, :] < indices[:, None])).astype(
            jnp.int32
        ),
        axis=1,
    )
    send_slot = targets * capacity + ranking
    slot_ids = jnp.arange(slot_count, dtype=jnp.int32)
    hit = send_slot[None, :] == slot_ids[:, None]
    block_of_slot = jnp.sum(jnp.where(hit, indices[None, :], 0), axis=1)
    pos_slots = jnp.sum(jnp.where(hit, curve_pos[None, :] + 1, 0), axis=1).astype(jnp.float32) - 1.0
    ocean = ice_mask > 0
    payload = jnp.stack([pack(surface_temp), pack(salinity)], axis=1)
    outgoing = payload[block_of_slot]
    incoming, in_pos = (
        lax.all_to_all(outgoing, "lon", split_axis=0, concat_axis=0, tiled=True),
        lax.all_to_all(pos_slots, "lon", split_axis=0, concat_axis=0, tiled=True),
    )
    local = in_pos.astype(jnp.int32) - lax.axis_index("lon") * block_count
    local = jnp.where(in_pos >= 0.0, local, block_count)
    arrive_slot = jnp.sum(
        jnp.where(local[None, :] == indices[:, None], slot_ids[None, :], 0), axis=1
    )
    arrived = incoming[arrive_slot]
    area_out, volume_out, coupled = thermo(
        ice_area, ice_volume, air_temp, arrived[:, 0], arrived[:, 1], ocean
    )
    replies = coupled[jnp.minimum(local, block_count - 1)]
    returned = lax.all_to_all(replies, "lon", split_axis=0, concat_axis=0, tiled=True)
    coupled_tile = returned[send_slot]
    mass = unpack(coupled_tile[:, 0])
    strength = unpack(coupled_tile[:, 1])
    velocity_out, stress_out = dynamics(
        velocity, stress, wind_stress, ocean_current, mass, strength
    )
    return (velocity_out, stress_out, area_out, volume_out)


def solution(mesh):
    return jax.shard_map(
        shards,
        mesh=mesh,
        in_specs=(
            P("grp", "lon"),
            P("grp", "lon"),
            P(None, "grp", "lon"),
            P(None, "grp", "lon"),
            P(None, "grp", "lon"),
            P(None, "grp", "lon"),
            P(("grp", "lon"), None, None),
            P(("grp", "lon"), None, None),
            P(("grp", "lon"), None),
            P(("grp", "lon")),
            P(("grp", "lon")),
        ),
        out_specs=(
            P(None, "grp", "lon"),
            P(None, "grp", "lon"),
            P(("grp", "lon"), None, None),
            P(("grp", "lon"), None, None),
        ),
        check_vma=False,
    )
```

time: 262 us -> 118 us (0.45); the launches traced: 258 us -> 117 us
  local copies, waits for them, and re-layouts: 87.7 us -> 14.9 us
  starting transfers between devices: 55.3 us -> 13.7 us
  waiting for transfers between devices: 91.1 us -> 52.7 us
  Pallas kernels: 0 us -> 29.9 us
  other arithmetic: 21.8 us -> 4.87 us
    ppermute x56 -> x0, waiting for transfers between devices: 65.5 us -> none  [the longest x24 31.8 us: swapped(): return lax.ppermute(block, axis, route)]
    scatter x20 -> x0, local copies, waits for them, and re-layouts: 48.8 us -> none  [the longest x16 38.7 us: extend(): return padded.at[:, -1, 1:-1].set(north).at[:, 0, 1:-1].set(south)]
    ppermute x56 -> x0, starting transfers between devices: 41.5 us -> none  [the longest x16 16.4 us: padded_2(): lax.ppermute(head, axis, [((i + 1) % count, i) for i in range(count)])]
    pallas_call x0 -> x1, Pallas kernels: none -> 29.9 us  [dynamics(): pl.pallas_call(functools.partial(dynamics_kernel, n_grp, n_lon), out_shap...]
    all_to_all x1, waiting for transfers between devices: 0.01 us -> 26.5 us  [shards(): lax.all_to_all(replies, 'lon', split_axis=0, concat_axis=0, tiled=True)]
    concatenate x8 -> x0, local copies, waits for them, and re-layouts: 14.2 us -> none  [padded_2(): jnp.concatenate([lax.ppermute(tail, axis, [(i, (i + 1) % count) for i in...]
    div x10 -> x0, other arithmetic: 8.4 us -> none  [the longest x3 2.55 us: subcycle(): sig_one = (stress[0] + RELAX * (ratio * divu - strength)) / (1.0 + RELAX)]
    rev x8 -> x0, local copies, waits for them, and re-layouts: 5.67 us -> none  [extend(): mirrored = signs[:, None] * partner[:, ::-1]]
  transfers between devices with their start and end apart: 59 -> 3, of which waited for: 35 -> 2; matrix products, arithmetic and copies ran while one was open for 12% -> 5% of each run, Pallas kernels for 0% -> 0%
where the time goes in v1:
time: 118 us; the launch traced here: 117 us
  waiting for transfers between devices  52.7 us (45%)
  Pallas kernels  29.9 us (25%)
  local copies, waits for them, and re-layouts  14.9 us (13%)
  starting transfers between devices  13.7 us (12%)
  other arithmetic  4.87 us (4%)
    pallas_call x1, Pallas kernels, dynamics(): pl.pallas_call(functools.partial(dynamics_kernel, n_grp, n_lon), out_shap...  29.9 us
    all_to_all x1, waiting for transfers between devices, shards(): lax.all_to_all(replies, 'lon', split_axis=0, concat_axis=0, tiled=True)  26.5 us
    all_to_all x1, waiting for transfers between devices, shards(): lax.all_to_all(outgoing, 'lon', split_axis=0, concat_axis=0, tiled=True)  26.2 us
    all_to_all x1, starting transfers between devices, shards(): lax.all_to_all(outgoing, 'lon', split_axis=0, concat_axis=0, tiled=True)  5.23 us
    all_to_all x1, starting transfers between devices, shards(): lax.all_to_all(pos_slots, 'lon', split_axis=0, concat_axis=0, tiled=True)  4.88 us
    all_to_all x1, starting transfers between devices, shards(): lax.all_to_all(replies, 'lon', split_axis=0, concat_axis=0, tiled=True)  3.56 us
    gather x1, local copies, waits for them, and re-layouts, shards(): replies = coupled[jnp.minimum(local, block_count - 1)]  2.59 us
    gather x1, local copies, waits for them, and re-layouts, shards(): outgoing = payload[block_of_slot]  2.57 us
  transfers between devices with their start and end apart: 3, of which 2 were waited for; matrix products, arithmetic and copies ran while one was open for 5% of the time, Pallas kernels for 0%

profile of v1, /device:TPU:6, one launch (start us, length us, event | category | flops | bytes accessed | tf_op | source)
XLA Modules:
  0.0 116.9 jit_solution(4690540959280645444)
XLA Ops:
  0.6 0.7 and_select_fusion
  1.3 0.2 convert_reduce_fusion
  1.6 0.7 sub.54
  2.3 4.9 %all-to-all-start.1 = ((f32[8,8,1]{1,2,0:T(1,128)}), f32[8,8,1]{1,2,0:T(1,128)S(1)}, u32[]{:S(2)}, u32[]{:S(2)}) async-start(f32[8,8,1]{1,2,0:T(1,128)} %bitcast.6), calls=%async_computation.1 | async-start | bytes 8192 | tf_op jit(solution)/shard_map/all_to_all | solution.py:348
  7.2 1.2 %stack_reshape.6 = f32[32,1,2048]{2,1,0:T(1,128)S(1)} reshape(f32[8,4,8,256]{3,2,1,0:T(8,128)} %bitcast.61) | data formatting | bytes 524288 | tf_op jit(solution)/shard_map/stack;reshape | solution.py:344
  8.4 1.2 %stack_reshape.7 = f32[32,1,2048]{2,1,0:T(1,128)S(1)} reshape(f32[8,4,8,256]{3,2,1,0:T(8,128)} %bitcast.62) | data formatting | bytes 524288 | tf_op jit(solution)/shard_map/stack;reshape | solution.py:344
  9.6 0.5 pad_maximum_fusion
  10.1 2.6 %gather_fusion = f32[64,2,2048]{2,1,0:T(2,128)} fusion(f32[32,2,2048]{2,1,0:T(2,128)S(1)} %pad_maximum_fusion, s32[1024]{0:T(1024)S(1)} %pad_clamp_fusion.3), kind=kCustom, calls=%fused_computation | custom fusion | bytes 2097408 | tf_op jit(solution)/shard_map/gather | solution.py:345
  12.7 5.2 %all-to-all-start = ((f32[64,2,2048]{2,1,0:T(2,128)}), f32[64,2,2048]{2,1,0:T(2,128)S(1)}, u32[]{:S(2)}, u32[]{:S(2)}) async-start(f32[64,2,2048]{2,1,0:T(2,128)} %gather_fusion), calls=%async_computation | async-start | bytes 2097152 | tf_op jit(solution)/shard_map/all_to_all | solution.py:347
  18.3 26.2 %all-to-all-done = f32[64,2,2048]{2,1,0:T(2,128)S(1)} async-done(((f32[64,2,2048]{2,1,0:T(2,128)}), f32[64,2,2048]{2,1,0:T(2,128)S(1)}, u32[]{:S(2)}, u32[]{:S(2)}) %all-to-all-start) | async-done | bytes 1048608 | tf_op jit(solution)/shard_map/all_to_all | solution.py:347
  44.5 1.1 gather_fusion.1
  45.6 0.9 multiply_exponential_fusion
  46.6 0.2 copy_bitcast_fusion
  46.9 0.4 copy-done.5
  47.3 2.0 %fusion.10 = (f32[32,2048]{1,0:T(8,128)S(1)}, f32[32,2048]{1,0:T(8,128)S(1)}, f32[32,5,2048]{2,0,1:T(8,128)}, f32[32,5,2048]{2,0,1:T(8,128)}) fusion(f32[32,2048]{1,0:T(8,128)S(1)} %get-tuple-element.28, f32[32,5,2048]{2,0,1:T(8,128)S(1)} %copy-done.4, f32[32,5,2048]{2,0,1:T(8,128)S(1)} %copy-done.5, f32[32,2048]{1,0:T(8,128)S(1)} %fusion, ...), kind=kLoop, calls=%fused_computation.56 | loop fusion | flops 3145728 | bytes 6553632 | tf_op jit(solution)/shard_map/reduce_sum | solution.py:39
  49.6 0.4 copy.20
  50.0 2.6 %gather_fusion.2 = f32[64,2,2048]{2,1,0:T(2,128)} fusion(f32[32,2,2048]{2,1,0:T(2,128)S(1)} %copy.20, s32[1024]{0:T(1024)S(1)} %pad_clamp_fusion.1), kind=kCustom, calls=%fused_computation.2 | custom fusion | bytes 2097408 | tf_op jit(solution)/shard_map/gather | solution.py:359
  52.6 3.6 %all-to-all-start.2 = ((f32[64,2,2048]{2,1,0:T(2,128)}), f32[64,2,2048]{2,1,0:T(2,128)S(1)}, u32[]{:S(2)}, u32[]{:S(2)}) async-start(f32[64,2,2048]{2,1,0:T(2,128)} %gather_fusion.2), calls=%async_computation.2 | async-start | bytes 2097152 | tf_op jit(solution)/shard_map/all_to_all | solution.py:360
  56.1 26.5 %all-to-all-done.2 = f32[64,2,2048]{2,1,0:T(2,128)S(1)} async-done(((f32[64,2,2048]{2,1,0:T(2,128)}), f32[64,2,2048]{2,1,0:T(2,128)S(1)}, u32[]{:S(2)}, u32[]{:S(2)}) %all-to-all-start.2) | async-done | bytes 1048608 | tf_op jit(solution)/shard_map/all_to_all | solution.py:360
  82.6 1.1 gather_fusion.3
  83.8 1.4 %slice_reduce_fusion = (f32[32,2048]{1,0:T(8,128)S(1)}, f32[32,2048]{1,0:T(8,128)S(1)}) fusion(f32[32,2,2048]{2,1,0:T(2,128)S(1)} %gather_fusion.3), kind=kLoop, calls=%fused_computation.10 | loop fusion | bytes 1048576 | tf_op jit(solution)/shard_map/slice | solution.py:363
  85.4 29.9 %dynamics.1 = (f32[2,64,1024]{2,1,0:T(8,128)S(1)}, f32[3,64,1024]{2,1,0:T(8,128)S(1)}) custom-call(f32[2,64,1024]{2,1,0:T(8,128)S(1)} %copy-done.1, f32[3,64,1024]{2,1,0:T(8,128)S(1)} %copy-done, f32[2,64,1024]{2,1,0:T(8,128)S(1)} %copy-done.2, f32[2,64,1024]{2,1,0:T(8,128)S(1)} %copy-done.3, f32[64,1024]{1,0:T(8,128)S(1)} %bitcast.57, f32[64,1024]{1,0:T(8,128)S(1)} %bitcast.58), custom_call_target="tpu_custom_call" | custom-call | tf_op jit(solution)/shard_map/dynamics/pallas_call | solution.py:286
  115.3 0.8 copy.31
  116.1 0.9 copy.32
  (36 shorter events, 1.0 us)
Async XLA Ops:
  2.3 10.4 %all-to-all-start.1 = ((f32[8,8,1]{1,2,0:T(1,128)}), f32[8,8,1]{1,2,0:T(1,128)S(1)}, u32[]{:S(2)}, u32[]{:S(2)}) async-start(f32[8,8,1]{1,2,0:T(1,128)} %bitcast.6), calls=%async_computation.1 | async-start | bytes 8192 | tf_op jit(solution)/shard_map/all_to_all | solution.py:348
  12.7 5.2 %copy-start.7 = (s32[32]{0:T(128)S(1)}, s32[32]{0:T(128)}, u32[]{:S(2)}) copy-start(s32[32]{0:T(128)} %param.20) | copy-start | bytes 388
  12.7 31.8 %all-to-all-start = ((f32[64,2,2048]{2,1,0:T(2,128)}), f32[64,2,2048]{2,1,0:T(2,128)S(1)}, u32[]{:S(2)}, u32[]{:S(2)}) async-start(f32[64,2,2048]{2,1,0:T(2,128)} %gather_fusion), calls=%async_computation | async-start | bytes 2097152 | tf_op jit(solution)/shard_map/all_to_all | solution.py:347
  44.5 2.2 %copy-start.6 = (f32[32,2048]{1,0:T(8,128)S(1)}, f32[32,2048]{1,0:T(8,128)}, u32[]{:S(2)}) copy-start(f32[32,2048]{1,0:T(8,128)} %param.19) | copy-start | bytes 786436
  45.6 1.3 %copy-start.4 = (f32[32,5,2048]{2,0,1:T(8,128)S(1)}, f32[32,5,2048]{2,0,1:T(8,128)}, u32[]{:S(2)}) copy-start(f32[32,5,2048]{2,0,1:T(8,128)} %param.18) | copy-start | bytes 3932164
  45.6 1.7 %copy-start.5 = (f32[32,5,2048]{2,0,1:T(8,128)S(1)}, f32[32,5,2048]{2,0,1:T(8,128)}, u32[]{:S(2)}) copy-start(f32[32,5,2048]{2,0,1:T(8,128)} %param.17) | copy-start | bytes 3932164
  52.6 30.1 %all-to-all-start.2 = ((f32[64,2,2048]{2,1,0:T(2,128)}), f32[64,2,2048]{2,1,0:T(2,128)S(1)}, u32[]{:S(2)}, u32[]{:S(2)}) async-start(f32[64,2,2048]{2,1,0:T(2,128)} %gather_fusion.2), calls=%async_computation.2 | async-start | bytes 2097152 | tf_op jit(solution)/shard_map/all_to_all | solution.py:360
  82.6 2.7 %copy-start.3 = (f32[2,64,1024]{2,1,0:T(8,128)S(1)}, f32[2,64,1024]{2,1,0:T(8,128)}, u32[]{:S(2)}) copy-start(f32[2,64,1024]{2,1,0:T(8,128)} %cur_ref.1) | copy-start | bytes 1572868
  83.8 1.6 %copy-start = (f32[3,64,1024]{2,1,0:T(8,128)S(1)}, f32[3,64,1024]{2,1,0:T(8,128)}, u32[]{:S(2)}) copy-start(f32[3,64,1024]{2,1,0:T(8,128)} %str_ref.1) | copy-start | bytes 2359300
  83.8 1.6 %copy-start.1 = (f32[2,64,1024]{2,1,0:T(8,128)S(1)}, f32[2,64,1024]{2,1,0:T(8,128)}, u32[]{:S(2)}) copy-start(f32[2,64,1024]{2,1,0:T(8,128)} %vel_ref.1) | copy-start | bytes 1572868
  83.8 1.6 %copy-start.2 = (f32[2,64,1024]{2,1,0:T(8,128)S(1)}, f32[2,64,1024]{2,1,0:T(8,128)}, u32[]{:S(2)}) copy-start(f32[2,64,1024]{2,1,0:T(8,128)} %wind_ref.1) | copy-start | bytes 1572868

commit v2 on v1

v2 whole, which is shorter than its diff:
```python
import functools

import jax
import jax.numpy as jnp
from jax import lax
from jax.experimental import pallas as pl
from jax.experimental.pallas import tpu as pltpu
from jax.sharding import PartitionSpec as P

BY = 8
BX = 256
SUB = 4

KAPPA = 0.02
MELT = 0.6
PSTAR = 10.0
CSTAR = 20.0
RELAX = 0.4
FCOR = 0.3

HALO = 2 * SUB
PAD = 8
LANES = 128
MESH = pl.DeviceIdType.MESH

N_FIELD = 9


def thermo(area, volume, air, temp_blocks, salt_blocks, ocean):
    freeze = -0.054 * salt_blocks
    excess = temp_blocks - freeze
    growth = KAPPA * area * (freeze - air)[:, None, :] / (volume + 0.1)
    vol_new = (volume + growth) * jnp.exp(-MELT * excess)[:, None, :]
    area_new = area * jnp.exp(-0.5 * MELT * excess)[:, None, :]
    keep = ocean[:, None, None]
    area_keep = jnp.where(keep, area_new, area)
    volume_keep = jnp.where(keep, vol_new, volume)
    return (area_keep, volume_keep)


def exact_dot(a, b):
    return jnp.dot(a, b, precision=lax.Precision.HIGHEST, preferred_element_type=jnp.float32)


def coupled_kernel(
    n_grp, n_lon, pos_row_ref, pos_col_ref, keep_ref, temp_ref, salt_ref, wind_ref, cur_ref,
    vel_ref, str_ref, area_ref, volume_ref, air_ref, vel_out, str_out, arrived_out,
    ext, inv, mir, out_e, out_w, in_w, in_e,
    blocks, flat, sums, slot_sums, pos_send, pos_recv, sea_send, sea_recv, ice_send, ice_recv,
    row_send, row_recv, col_send, col_recv, a2a_send, a2a_recv,
):
    rows, cols = temp_ref.shape
    wide = cols + LANES
    top = PAD + HALO
    tall = rows + 2 * HALO
    n_block, cells = air_ref.shape
    cap = sea_send.shape[2]
    n_slot = n_lon * cap
    g = lax.axis_index("grp")
    l = lax.axis_index("lon")
    east = lax.rem(l + 1, n_lon)
    west = lax.rem(l + n_lon - 1, n_lon)
    mirror = n_lon - 1 - l
    not_south = g > 0
    not_north = g < n_grp - 1

    barrier = pltpu.get_barrier_semaphore()

    def peer(d):
        return lax.rem(l + d, n_lon)

    def source(d):
        return lax.rem(l + n_lon - d, n_lon)

    for d in range(1, n_lon):
        pl.semaphore_signal(
            barrier, inc=1, device_id={"grp": g, "lon": peer(d)}, device_id_type=MESH
        )

    @pl.when(not_south)
    def _():
        pl.semaphore_signal(
            barrier, inc=1, device_id={"grp": g - 1, "lon": l}, device_id_type=MESH
        )

    @pl.when(not_north)
    def _():
        pl.semaphore_signal(
            barrier, inc=1, device_id={"grp": g + 1, "lon": l}, device_id_type=MESH
        )

    near = sorted(range(1, n_lon), key=lambda d: (min(d, n_lon - d), d))
    far = near[::-1]

    pos_row = pos_row_ref[...]
    to_row = jnp.floor(pos_row * (1.0 / n_block))
    to_col = jnp.floor(pos_col_ref[...] * (1.0 / n_block))
    down = lax.broadcasted_iota(jnp.int32, (n_block, n_block), 0)
    along = lax.broadcasted_iota(jnp.int32, (n_block, n_block), 1)
    same = to_col == to_row
    rank_row = jnp.sum(jnp.where(same & (down < along), 1.0, 0.0), axis=0, keepdims=True)
    rank_col = jnp.sum(jnp.where(same & (along < down), 1.0, 0.0), axis=1, keepdims=True)
    slot_row = to_row * cap + rank_row
    slot_col = to_col * cap + rank_col
    slot_down = lax.broadcasted_iota(jnp.int32, (n_slot, n_block), 0).astype(jnp.float32)
    slot_along = lax.broadcasted_iota(jnp.int32, (n_block, n_slot), 1).astype(jnp.float32)
    to_slots = jnp.where(slot_down == slot_row, 1.0, 0.0)
    from_slots = jnp.where(slot_along == slot_col, 1.0, 0.0)
    pos_slot = jnp.sum(to_slots * (pos_row + 1.0), axis=1, keepdims=True) - 1.0
    pos_wide = jnp.broadcast_to(pos_slot, (n_slot, LANES))
    for p in range(n_lon):
        pos_send[p] = pos_wide[p * cap : (p + 1) * cap]

    for f, ref in enumerate((temp_ref, salt_ref)):
        for i in range(rows):
            for c in range(cols // BX):
                blocks[f, pl.ds((i // BY) * (cols // BX) + c, 1), pl.ds((i % BY) * BX, BX)] = ref[
                    pl.ds(i, 1), pl.ds(c * BX, BX)
                ]
    for f in range(2):
        packed = exact_dot(to_slots, blocks[f])
        for p in range(n_lon):
            sea_send[p, f] = packed[p * cap : (p + 1) * cap]

    pl.semaphore_wait(
        barrier, n_lon - 1 + jnp.where(not_south, 1, 0) + jnp.where(not_north, 1, 0)
    )

    def lon_copy(kind, src, dst, d):
        return pltpu.make_async_remote_copy(
            src_ref=src.at[peer(d)], dst_ref=dst.at[l],
            send_sem=a2a_send.at[kind, d], recv_sem=a2a_recv.at[kind, d],
            device_id={"grp": g, "lon": peer(d)}, device_id_type=MESH,
        )

    pos_copy = {d: lon_copy(0, pos_send, pos_recv, d) for d in near}
    sea_copy = {d: lon_copy(1, sea_send, sea_recv, d) for d in near}
    ice_copy = {d: lon_copy(2, ice_send, ice_recv, d) for d in near}
    for d in far:
        pos_copy[d].start()
    for d in far:
        sea_copy[d].start()
    pos_recv[l] = pos_send[l]
    sea_recv[l] = sea_send[l]

    body = pl.ds(top, rows)
    main = pl.ds(0, cols)
    for f in range(2):
        ext[f, body, main] = vel_ref[f]
        ext[5 + f, body, main] = wind_ref[f] + cur_ref[f]
    for f in range(3):
        ext[2 + f, body, main] = str_ref[f]
    for f in range(N_FIELD):
        ext[f, pl.ds(0, PAD), :] = jnp.zeros((PAD, wide), jnp.float32)
        ext[f, pl.ds(top + rows + HALO, PAD), :] = jnp.zeros((PAD, wide), jnp.float32)

    @pl.when(jnp.logical_not(not_south))
    def _():
        for f in range(N_FIELD):
            ext[f, pl.ds(PAD, HALO), main] = jnp.zeros((HALO, cols), jnp.float32)

    lane = lax.broadcasted_iota(jnp.int32, (tall, LANES), 1)
    span = pl.ds(PAD, tall)

    def row_start(part, lo, n):
        fs = pl.ds(lo, n)

        @pl.when(jnp.logical_not(not_north))
        def _():
            a = lax.broadcasted_iota(jnp.int32, (LANES, LANES), 0)
            b = lax.broadcasted_iota(jnp.int32, (LANES, LANES), 1)
            flip = (a + b == LANES - 1).astype(jnp.float32)
            for f in range(lo, lo + n):
                sign = -1.0 if f in (0, 1, 5, 6) else 1.0
                for c in range(cols // LANES):
                    x = ext[f, pl.ds(top + rows - HALO, HALO), pl.ds(c * LANES, LANES)]
                    y = sign * exact_dot(x, flip)
                    for r in range(HALO):
                        mir[f, pl.ds(HALO - 1 - r, 1), pl.ds(cols - (c + 1) * LANES, LANES)] = y[
                            r : r + 1
                        ]

        low = ext.at[fs, pl.ds(PAD, HALO), main]
        high = ext.at[fs, pl.ds(top + rows, HALO), main]
        to_south = pltpu.make_async_remote_copy(
            src_ref=ext.at[fs, pl.ds(top, HALO), main], dst_ref=high,
            send_sem=row_send.at[part, 0], recv_sem=row_recv.at[part, 0],
            device_id={"grp": jnp.where(not_south, g - 1, g), "lon": l}, device_id_type=MESH,
        )
        to_north = pltpu.make_async_remote_copy(
            src_ref=ext.at[fs, pl.ds(top + rows - HALO, HALO), main], dst_ref=low,
            send_sem=row_send.at[part, 1], recv_sem=row_recv.at[part, 1],
            device_id={"grp": jnp.where(not_north, g + 1, g), "lon": l}, device_id_type=MESH,
        )
        to_mirror = pltpu.make_async_remote_copy(
            src_ref=mir.at[fs], dst_ref=high,
            send_sem=row_send.at[part, 1], recv_sem=row_recv.at[part, 0],
            device_id={"grp": g, "lon": mirror}, device_id_type=MESH,
        )

        @pl.when(not_south)
        def _():
            to_south.start()

        @pl.when(not_north)
        def _():
            to_north.start()

        @pl.when(jnp.logical_not(not_north))
        def _():
            to_mirror.start()

        return to_south, to_north, to_mirror

    def row_finish(copies):
        to_south, to_north, to_mirror = copies
        to_south.wait_recv()

        @pl.when(not_south)
        def _():
            to_north.wait_recv()

        @pl.when(not_south)
        def _():
            to_south.wait_send()

        @pl.when(not_north)
        def _():
            to_north.wait_send()

        @pl.when(jnp.logical_not(not_north))
        def _():
            to_mirror.wait_send()

    def col_start(part, lo, n):
        east_pack = jnp.zeros((tall, LANES), jnp.float32)
        west_pack = jnp.zeros((tall, LANES), jnp.float32)
        for k in range(n):
            here = (lane >= k * HALO) & (lane < (k + 1) * HALO)
            tail = ext[lo + k, span, pl.ds(cols - LANES, LANES)]
            head = ext[lo + k, span, pl.ds(0, LANES)]
            east_pack = jnp.where(here, pltpu.roll(tail, (k + 1) * HALO, 1), east_pack)
            west_pack = jnp.where(here, pltpu.roll(head, k * HALO, 1) if k else head, west_pack)
        out_e[part] = east_pack
        out_w[part] = west_pack
        to_east = pltpu.make_async_remote_copy(
            src_ref=out_e.at[part], dst_ref=in_w.at[part],
            send_sem=col_send.at[part, 0], recv_sem=col_recv.at[part, 0],
            device_id={"grp": g, "lon": east}, device_id_type=MESH,
        )
        to_west = pltpu.make_async_remote_copy(
            src_ref=out_w.at[part], dst_ref=in_e.at[part],
            send_sem=col_send.at[part, 1], recv_sem=col_recv.at[part, 1],
            device_id={"grp": g, "lon": west}, device_id_type=MESH,
        )
        to_east.start()
        to_west.start()
        return to_east, to_west

    def col_finish(part, lo, n, copies):
        for copy in copies:
            copy.wait()
        from_west = in_w[part]
        from_east = in_e[part]
        for k in range(n):
            e = pltpu.roll(from_east, LANES - k * HALO, 1) if k else from_east
            w = pltpu.roll(from_west, LANES - (k + 1) * HALO, 1)
            ext[lo + k, span, pl.ds(cols, LANES)] = jnp.where(
                lane < HALO, e, jnp.where(lane >= LANES - HALO, w, 0.0)
            )

    early_rows = row_start(0, 0, 7)

    keep = keep_ref[...] > 0.0
    n_cat = area_ref.shape[0]
    chunk = 512

    def reduce_chunk(i, carry):
        at = pl.ds(pl.multiple_of(i * chunk, chunk), chunk)
        area_sum = jnp.zeros((n_block, chunk), jnp.float32)
        vol_sum = jnp.zeros((n_block, chunk), jnp.float32)
        rate = jnp.zeros((n_block, chunk), jnp.float32)
        for c in range(n_cat):
            area = area_ref[c, :, at]
            vol = volume_ref[c, :, at]
            area_sum = area_sum + area
            vol_sum = vol_sum + vol
            rate = rate + area / (vol + 0.1)
        rate = KAPPA * rate
        sums[0, :, at] = jnp.where(keep, area_sum, 0.0)
        sums[1, :, at] = jnp.where(keep, vol_sum - rate * air_ref[:, at], 0.0)
        sums[2, :, at] = jnp.where(keep, rate, 0.0)
        return carry

    lax.fori_loop(0, cells // chunk, reduce_chunk, 0)

    for d in near:
        pos_copy[d].wait_recv()
    base = (l * n_block).astype(jnp.float32)
    for p in range(n_lon):
        flat[pl.ds(p * cap, cap), pl.ds(0, LANES)] = pos_recv[p]
    local = flat[:, pl.ds(0, LANES)] - base
    block_along = lax.broadcasted_iota(jnp.int32, (n_slot, LANES), 1).astype(jnp.float32)
    at_slot = jnp.where((local == block_along) & (block_along < n_block), 1.0, 0.0)
    for f in range(3):
        gathered = exact_dot(at_slot[:, :n_block], sums[f])
        for p in range(n_lon):
            slot_sums[p, f] = gathered[p * cap : (p + 1) * cap]

    row_finish(early_rows)
    early_cols = col_start(0, 0, 7)

    def answer(p):
        freeze = -0.054 * sea_recv[p, 1]
        decay = jnp.exp((-0.5 * MELT) * (sea_recv[p, 0] - freeze))
        mass = (slot_sums[p, 1] + slot_sums[p, 2] * freeze) * (decay * decay)
        conc = slot_sums[p, 0] * decay
        return mass, PSTAR * mass * jnp.exp(-CSTAR * (1.0 - conc))

    own_mass, own_strength = answer(l)
    ice_recv[l, 0] = own_mass
    ice_recv[l, 1] = own_strength
    for d in near:
        sea_copy[d].wait_recv()
        mass, strength = answer(source(d))
        ice_send[source(d), 0] = mass
        ice_send[source(d), 1] = strength
        ice_copy[n_lon - d].start()

    col_finish(0, 0, 7, early_cols)

    for f in range(2):
        for p in range(n_lon):
            flat[pl.ds(p * cap, cap), :] = sea_recv[p, f]
        arrived_out[f] = lax.dot_general(
            at_slot, flat[...], (((0,), (0,)), ((), ())),
            precision=lax.Precision.HIGHEST, preferred_element_type=jnp.float32,
        )[:n_block]

    for d in near:
        ice_copy[d].wait_recv()
    for f in range(2):
        for p in range(n_lon):
            flat[pl.ds(p * cap, cap), :] = ice_recv[p, f]
        blocks[f] = exact_dot(from_slots, flat[...])
        for i in range(rows):
            for c in range(cols // BX):
                ext[7 + f, pl.ds(top + i, 1), pl.ds(c * BX, BX)] = blocks[
                    f, pl.ds((i // BY) * (cols // BX) + c, 1), pl.ds((i % BY) * BX, BX)
                ]
    row_finish(row_start(1, 7, 2))
    col_finish(1, 7, 2, col_start(1, 7, 2))
    for d in near:
        pos_copy[d].wait_send()
        sea_copy[d].wait_send()
        ice_copy[d].wait_send()

    inv[...] = 1.0 / (2.0 * ext[7, span, :] + 1.0)

    @pl.when(jnp.logical_not(not_south))
    def _():
        inv[pl.ds(0, HALO), :] = jnp.zeros((HALO, wide), jnp.float32)

    def across(x):
        return pltpu.roll(x, wide - 1, 1) - pltpu.roll(x, 1, 1)

    sub = lax.broadcasted_iota(jnp.int32, (8, wide), 0)
    is_first = sub == 0
    is_last = sub == 7

    def three(f, r):
        return (
            ext[f, pl.ds(pl.multiple_of(r - 8, 8), 8), :],
            ext[f, pl.ds(r, 8), :],
            ext[f, pl.ds(pl.multiple_of(r + 8, 8), 8), :],
        )

    def upward(strips):
        below, here, above = strips
        return pltpu.roll(jnp.where(is_first, above, here), 7, 0) - pltpu.roll(
            jnp.where(is_last, below, here), 1, 0
        )

    scale = 1.0 / (1.0 + RELAX)

    def stress_strip(i, carry):
        r = pl.multiple_of(PAD + i * 8, 8)
        at = pl.ds(r, 8)
        u = three(0, r)
        v = three(1, r)
        u_y, v_y, u_x, v_x = upward(u), upward(v), across(u[1]), across(v[1])
        divu = (u_x + v_y) * 0.5
        tension = (u_x - v_y) * 0.5
        shear = (u_y + v_x) * 0.5
        square = divu * divu + (tension * tension + shear * shear) * 0.25 + 0.01
        strength = ext[8, at, :]
        ratio = strength * lax.rsqrt(square)
        ext[2, at, :] = (ext[2, at, :] + RELAX * (ratio * divu - strength)) * scale
        ratio = ratio * scale
        ext[3, at, :] = ext[3, at, :] * scale + (RELAX / 4.0) * (ratio * tension)
        ext[4, at, :] = ext[4, at, :] * scale + (RELAX / 8.0) * (ratio * shear)
        return carry

    def speed_strip(i, carry):
        r = pl.multiple_of(PAD + i * 8, 8)
        at = pl.ds(r, 8)
        one = three(2, r)
        two = three(3, r)
        mixed = three(4, r)
        s_x = across(one[1] + two[1])
        s_y = upward([x - y for x, y in zip(one, two)])
        c_x = across(mixed[1])
        c_y = upward(mixed)
        force_x = s_x * 0.25 + c_y * 0.5
        force_y = c_x * 0.5 + s_y * 0.25
        mass = ext[7, at, :]
        factor = inv[pl.ds(pl.multiple_of(i * 8, 8), 8), :]
        u = ext[0, at, :]
        v = ext[1, at, :]
        turn = FCOR * mass
        inertia = 2.0 * mass
        ext[0, at, :] = (inertia * u + force_x + ext[5, at, :] + turn * v) * factor
        ext[1, at, :] = (inertia * v + force_y + ext[6, at, :] - turn * u) * factor
        return carry

    def step(k, carry):
        lax.fori_loop(0, tall // 8, stress_strip, 0)
        lax.fori_loop(0, tall // 8, speed_strip, 0)
        return carry

    lax.fori_loop(0, SUB, step, 0)

    for f in range(2):
        vel_out[f] = ext[f, body, main]
    for f in range(3):
        str_out[f] = ext[2 + f, body, main]


def shards(
    surface_temp, salinity, wind_stress, ocean_current, velocity, stress,
    ice_area, ice_volume, air_temp, ice_mask, curve_pos,
):
    n_grp = lax.axis_size("grp")
    n_lon = lax.axis_size("lon")
    rows, cols = surface_temp.shape
    n_block, n_cat, cells = ice_area.shape
    cap = 2 * n_block // n_lon
    n_slot = n_lon * cap
    wide = cols + LANES
    tall = rows + 2 * HALO
    pos = curve_pos.astype(jnp.float32)
    ocean = ice_mask > 0
    f32 = functools.partial(pltpu.VMEM, dtype=jnp.float32)
    vmem = pl.BlockSpec(memory_space=pltpu.VMEM)
    velocity_out, stress_out, arrived = pl.pallas_call(
        functools.partial(coupled_kernel, n_grp, n_lon),
        out_shape=(
            jax.ShapeDtypeStruct(velocity.shape, jnp.float32),
            jax.ShapeDtypeStruct(stress.shape, jnp.float32),
            jax.ShapeDtypeStruct((2, n_block, cells), jnp.float32),
        ),
        in_specs=[vmem] * 12,
        out_specs=(vmem, vmem, vmem),
        scratch_shapes=[
            f32((N_FIELD, tall + 2 * PAD, wide)),
            f32((tall, wide)),
            f32((N_FIELD, HALO, cols)),
            f32((2, tall, LANES)),
            f32((2, tall, LANES)),
            f32((2, tall, LANES)),
            f32((2, tall, LANES)),
            f32((2, n_block, cells)),
            f32((n_slot, cells)),
            f32((3, n_block, cells)),
            f32((n_lon, 3, cap, cells)),
            f32((n_lon, cap, LANES)),
            f32((n_lon, cap, LANES)),
            f32((n_lon, 2, cap, cells)),
            f32((n_lon, 2, cap, cells)),
            f32((n_lon, 2, cap, cells)),
            f32((n_lon, 2, cap, cells)),
            pltpu.SemaphoreType.DMA((2, 2)),
            pltpu.SemaphoreType.DMA((2, 2)),
            pltpu.SemaphoreType.DMA((2, 2)),
            pltpu.SemaphoreType.DMA((2, 2)),
            pltpu.SemaphoreType.DMA((3, n_lon)),
            pltpu.SemaphoreType.DMA((3, n_lon)),
        ],
        compiler_params=pltpu.CompilerParams(
            collective_id=1, has_side_effects=True, vmem_limit_bytes=48 << 20
        ),
        name="coupled",
    )(
        pos[None, :], pos[:, None], ocean.astype(jnp.float32)[:, None],
        surface_temp, salinity, wind_stress, ocean_current, velocity, stress,
        ice_area.transpose(1, 0, 2), ice_volume.transpose(1, 0, 2), air_temp,
    )
    area_out, volume_out = thermo(
        ice_area, ice_volume, air_temp, arrived[0], arrived[1], ocean
    )
    return (velocity_out, stress_out, area_out, volume_out)


def solution(mesh):
    return jax.shard_map(
        shards,
        mesh=mesh,
        in_specs=(
            P("grp", "lon"),
            P("grp", "lon"),
            P(None, "grp", "lon"),
            P(None, "grp", "lon"),
            P(None, "grp", "lon"),
            P(None, "grp", "lon"),
            P(("grp", "lon"), None, None),
            P(("grp", "lon"), None, None),
            P(("grp", "lon"), None),
            P(("grp", "lon")),
            P(("grp", "lon")),
        ),
        out_specs=(
            P(None, "grp", "lon"),
            P(None, "grp", "lon"),
            P(("grp", "lon"), None, None),
            P(("grp", "lon"), None, None),
        ),
        check_vma=False,
    )
```

time: 118 us -> 101 us (0.86)
  Pallas kernels: 29.9 us -> 86.2 us
  waiting for transfers between devices: 52.7 us -> 0 us
  starting transfers between devices: 13.7 us -> 0 us
  local copies, waits for them, and re-layouts: 14.9 us -> 10.1 us
  other arithmetic: 4.87 us -> 3.39 us
    pallas_call x1, Pallas kernels: 29.9 us -> 86.2 us  [shards(): pl.pallas_call(functools.partial(coupled_kernel, n_grp, n_lon), out_shape...]
    all_to_all x3 -> x0, waiting for transfers between devices: 52.7 us -> none  [the longest x1 26.5 us: shards(): lax.all_to_all(replies, 'lon', split_axis=0, concat_axis=0, tiled=True)]
    all_to_all x3 -> x0, starting transfers between devices: 13.7 us -> none  [the longest x1 5.23 us: shards(): lax.all_to_all(outgoing, 'lon', split_axis=0, concat_axis=0, tiled=True)]
    unnamed x21 -> x20, local copies, waits for them, and re-layouts: 2.51 us -> 9.96 us
    gather x4 -> x0, local copies, waits for them, and re-layouts: 7.37 us -> none  [the longest x1 2.59 us: shards(): replies = coupled[jnp.minimum(local, block_count - 1)]]
    another operation x3 -> x0, local copies, waits for them, and re-layouts: 2.84 us -> none  [the longest x2 2.43 us: shards(): payload = jnp.stack([pack(surface_temp), pack(salinity)], axis=1)]
    reduce_sum x4 -> x0, other arithmetic: 2.43 us -> none  [the longest x1 2.04 us: thermo(): mass_sum = jnp.sum(vol_new, axis=1)]
    slice x1 -> x0, local copies, waits for them, and re-layouts: 1.36 us -> none  [shards(): strength = unpack(coupled_tile[:, 1])]
  transfers between devices with their start and end apart: 3 -> 0, of which waited for: 2 -> 0; matrix products, arithmetic and copies ran while one was open for 5% -> 0% of each run, Pallas kernels for 0% -> 0%
where the time goes in v2:
time: 101 us; the launch traced here: 100 us
  Pallas kernels  86.2 us (85%)
  local copies, waits for them, and re-layouts  10.1 us (10%)
  other arithmetic  3.39 us (3%)
    pallas_call x1, Pallas kernels, shards(): pl.pallas_call(functools.partial(coupled_kernel, n_grp, n_lon), out_shape...  86.2 us
    unnamed x20, local copies, waits for them, and re-layouts  9.96 us

profile of v2, /device:TPU:6, one launch (start us, length us, event | category | flops | bytes accessed | tf_op | source)
XLA Modules:
  0.0 100.4 jit_solution(3610861015084869328)
XLA Ops:
  0.6 0.7 broadcast_compare_fusion
  1.3 0.7 convert_bitcast_fusion.1
  1.9 0.1 copy.15.pos_col_ref
  2.0 0.1 copy.16.keep_ref
  2.1 0.0 copy-start
  2.1 0.9 copy-done
  3.1 0.0 copy-start.1
  3.1 1.1 %copy-done.1 = f32[3,64,1024]{2,1,0:T(8,128)S(1)} copy-done((f32[3,64,1024]{2,1,0:T(8,128)S(1)}, f32[3,64,1024]{2,1,0:T(8,128)}, u32[]{:S(2)}) %copy-start.1) | copy-done | bytes 786456
  4.2 0.0 copy-start.2
  4.2 1.0 %copy-done.2 = f32[2,64,1024]{2,1,0:T(8,128)S(1)} copy-done((f32[2,64,1024]{2,1,0:T(8,128)S(1)}, f32[2,64,1024]{2,1,0:T(8,128)}, u32[]{:S(2)}) %copy-start.2) | copy-done | bytes 524312
  5.3 0.0 copy-start.3
  5.3 1.0 %copy-done.3 = f32[2,64,1024]{2,1,0:T(8,128)S(1)} copy-done((f32[2,64,1024]{2,1,0:T(8,128)S(1)}, f32[2,64,1024]{2,1,0:T(8,128)}, u32[]{:S(2)}) %copy-start.3) | copy-done | bytes 524312
  6.3 0.0 copy-start.4
  6.3 1.0 %copy-done.4 = f32[2,64,1024]{2,1,0:T(8,128)S(1)} copy-done((f32[2,64,1024]{2,1,0:T(8,128)S(1)}, f32[2,64,1024]{2,1,0:T(8,128)}, u32[]{:S(2)}) %copy-start.4) | copy-done | bytes 524312
  7.3 0.9 copy-done.5
  8.3 0.9 copy-done.6
  9.2 86.2 %coupled.1 = (f32[2,64,1024]{2,1,0:T(8,128)S(1)}, f32[3,64,1024]{2,1,0:T(8,128)S(1)}, f32[2,32,2048]{2,1,0:T(8,128)S(1)}) custom-call(f32[1,32]{1,0:T(1,128)S(1)} %get-tuple-element.18.pos_row_ref, f32[32,1]{1,0:T(8,128)S(1)} %copy.15.pos_col_ref, f32[32,1]{1,0:T(8,128)S(1)} %copy.16.keep_ref, f32[64,1024]{1,0:T(8,128)S(1)} %copy-done.5, ...), custom_call_target="tpu_custom_call" | custom-call | tf_op jit(solution)/shard_map/coupled/pallas_call | solution.py:455
  95.5 0.0 copy-start.7
  95.5 0.1 fusion
  95.6 0.0 copy-done.8
  95.6 1.2 %copy-done.7 = f32[32,5,2048]{2,0,1:T(8,128)S(1)} copy-done((f32[32,5,2048]{2,0,1:T(8,128)S(1)}, f32[32,5,2048]{2,0,1:T(8,128)}, u32[]{:S(2)}) %copy-start.7) | copy-done | bytes 1310744
  96.8 2.0 %multiply_select_fusion.1 = (f32[32,5,2048]{2,0,1:T(8,128)}, f32[32,5,2048]{2,0,1:T(8,128)}) fusion(f32[32,5,2048]{2,0,1:T(8,128)S(1)} %copy-done.8, f32[32,5,2048]{2,0,1:T(8,128)S(1)} %copy-done.7, f32[32,2048]{1,0:T(8,128)S(1)} %get-tuple-element.13, f32[32,2048]{1,0:T(8,128)S(1)} %get-tuple-element.12, pred[32]{0:T(512)(128)(4,1)S(1)} %get-tuple-element.15, ...), kind=kLoop, calls=%fused_computation.1 | loop fusion | flops 2621440 | bytes 6029344 | tf_op jit(solution)/shard_map/jit(_where)/select_n | solution.py:37
  98.7 0.8 copy.19
  99.5 0.9 copy.20
  (3 shorter events, 0.0 us)
Async XLA Ops:
  2.1 0.9 copy-start
  3.1 1.1 %copy-start.1 = (f32[3,64,1024]{2,1,0:T(8,128)S(1)}, f32[3,64,1024]{2,1,0:T(8,128)}, u32[]{:S(2)}) copy-start(f32[3,64,1024]{2,1,0:T(8,128)} %str_ref.1) | copy-start | bytes 2359300
  4.2 1.0 %copy-start.2 = (f32[2,64,1024]{2,1,0:T(8,128)S(1)}, f32[2,64,1024]{2,1,0:T(8,128)}, u32[]{:S(2)}) copy-start(f32[2,64,1024]{2,1,0:T(8,128)} %wind_ref.1) | copy-start | bytes 1572868
  5.3 1.0 %copy-start.3 = (f32[2,64,1024]{2,1,0:T(8,128)S(1)}, f32[2,64,1024]{2,1,0:T(8,128)}, u32[]{:S(2)}) copy-start(f32[2,64,1024]{2,1,0:T(8,128)} %cur_ref.1) | copy-start | bytes 1572868
  6.3 1.0 %copy-start.4 = (f32[2,64,1024]{2,1,0:T(8,128)S(1)}, f32[2,64,1024]{2,1,0:T(8,128)}, u32[]{:S(2)}) copy-start(f32[2,64,1024]{2,1,0:T(8,128)} %vel_ref.1) | copy-start | bytes 1572868
  7.3 0.9 copy-start.5
  8.3 0.9 copy-start.6
  9.2 86.4 %copy-start.8 = (f32[32,5,2048]{2,0,1:T(8,128)S(1)}, f32[32,5,2048]{2,0,1:T(8,128)}, u32[]{:S(2)}) copy-start(f32[32,5,2048]{2,0,1:T(8,128)} %param.18) | copy-start | bytes 3932164
  95.5 1.3 %copy-start.7 = (f32[32,5,2048]{2,0,1:T(8,128)S(1)}, f32[32,5,2048]{2,0,1:T(8,128)}, u32[]{:S(2)}) copy-start(f32[32,5,2048]{2,0,1:T(8,128)} %param.17) | copy-start | bytes 3932164

commit v3 on v2

--- a/solution.py
+++ b/solution.py
@@ -43,9 +43,9 @@
 
 
 def coupled_kernel(
-    n_grp, n_lon, pos_row_ref, pos_col_ref, keep_ref, temp_ref, salt_ref, wind_ref, cur_ref,
-    vel_ref, str_ref, area_ref, volume_ref, air_ref, vel_out, str_out, arrived_out,
-    ext, inv, mir, out_e, out_w, in_w, in_e,
+    n_grp, n_lon, pos_ref, mask_ref, temp_hbm, salt_hbm, wind_hbm, cur_hbm,
+    vel_hbm, str_hbm, area_hbm, volume_hbm, air_hbm, vel_out, str_out, arrived_out,
+    temp_ref, salt_ref, wind_ref, cur_ref, area_ref, volume_ref, air_ref, load_sem, ext, inv, mir, out_e, out_w, in_w, in_e,
     blocks, flat, sums, slot_sums, pos_send, pos_recv, sea_send, sea_recv, ice_send, ice_recv,
     row_send, row_recv, col_send, col_recv, a2a_send, a2a_recv,
 ):
@@ -89,14 +89,40 @@
             barrier, inc=1, device_id={"grp": g + 1, "lon": l}, device_id_type=MESH
         )
 
+    body = pl.ds(top, rows)
+    main = pl.ds(0, cols)
+    loads = [
+        pltpu.make_async_copy(src, dst, load_sem.at[k])
+        for k, (src, dst) in enumerate(
+            (
+                (temp_hbm, temp_ref),
+                (salt_hbm, salt_ref),
+                (vel_hbm, ext.at[pl.ds(0, 2), body, main]),
+                (str_hbm, ext.at[pl.ds(2, 3), body, main]),
+                (wind_hbm, wind_ref),
+                (cur_hbm, cur_ref),
+                (area_hbm, area_ref),
+                (volume_hbm, volume_ref),
+                (air_hbm, air_ref),
+            )
+        )
+    ]
+    for load in loads:
+        load.start()
+
     near = sorted(range(1, n_lon), key=lambda d: (min(d, n_lon - d), d))
     far = near[::-1]
 
-    pos_row = pos_row_ref[...]
-    to_row = jnp.floor(pos_row * (1.0 / n_block))
-    to_col = jnp.floor(pos_col_ref[...] * (1.0 / n_block))
+    pos_row = pos_ref[...].astype(jnp.float32)
     down = lax.broadcasted_iota(jnp.int32, (n_block, n_block), 0)
     along = lax.broadcasted_iota(jnp.int32, (n_block, n_block), 1)
+
+    def column(row):
+        return jnp.sum(jnp.where(down == along, row, 0.0), axis=1, keepdims=True)
+
+    keep = column(mask_ref[...].astype(jnp.float32)) > 0.0
+    to_row = jnp.floor(pos_row * (1.0 / n_block))
+    to_col = column(to_row)
     same = to_col == to_row
     rank_row = jnp.sum(jnp.where(same & (down < along), 1.0, 0.0), axis=0, keepdims=True)
     rank_col = jnp.sum(jnp.where(same & (along < down), 1.0, 0.0), axis=1, keepdims=True)
@@ -111,6 +137,8 @@
     for p in range(n_lon):
         pos_send[p] = pos_wide[p * cap : (p + 1) * cap]
 
+    loads[0].wait()
+    loads[1].wait()
     for f, ref in enumerate((temp_ref, salt_ref)):
         for i in range(rows):
             for c in range(cols // BX):
@@ -143,13 +171,10 @@
     pos_recv[l] = pos_send[l]
     sea_recv[l] = sea_send[l]
 
-    body = pl.ds(top, rows)
-    main = pl.ds(0, cols)
+    for load in loads[2:6]:
+        load.wait()
     for f in range(2):
-        ext[f, body, main] = vel_ref[f]
         ext[5 + f, body, main] = wind_ref[f] + cur_ref[f]
-    for f in range(3):
-        ext[2 + f, body, main] = str_ref[f]
     for f in range(N_FIELD):
         ext[f, pl.ds(0, PAD), :] = jnp.zeros((PAD, wide), jnp.float32)
         ext[f, pl.ds(top + rows + HALO, PAD), :] = jnp.zeros((PAD, wide), jnp.float32)
@@ -170,15 +195,27 @@
             a = lax.broadcasted_iota(jnp.int32, (LANES, LANES), 0)
             b = lax.broadcasted_iota(jnp.int32, (LANES, LANES), 1)
             flip = (a + b == LANES - 1).astype(jnp.float32)
-            for f in range(lo, lo + n):
-                sign = -1.0 if f in (0, 1, 5, 6) else 1.0
-                for c in range(cols // LANES):
-                    x = ext[f, pl.ds(top + rows - HALO, HALO), pl.ds(c * LANES, LANES)]
-                    y = sign * exact_dot(x, flip)
-                    for r in range(HALO):
-                        mir[f, pl.ds(HALO - 1 - r, 1), pl.ds(cols - (c + 1) * LANES, LANES)] = y[
-                            r : r + 1
-                        ]
+            count = cols // LANES
+            edge = pl.ds(top + rows - HALO, HALO)
+            x = jnp.concatenate(
+                [
+                    ext[fs, edge, pl.ds(c * LANES, LANES)].reshape(n * HALO, LANES)
+                    for c in range(count)
+                ],
+                axis=0,
+            )
+            y = exact_dot(x, flip).reshape(count * n, HALO, LANES)
+            row = lax.broadcasted_iota(jnp.int32, (count * n, HALO, LANES), 1)
+            for step in (1, 2, 4):
+                y = jnp.where(
+                    row % (2 * step) < step,
+                    pltpu.roll(y, HALO - step, 1),
+                    pltpu.roll(y, step, 1),
+                )
+            for c in range(count):
+                for k in range(n):
+                    sign = -1.0 if lo + k in (0, 1, 5, 6) else 1.0
+                    mir[lo + k, :, pl.ds(cols - (c + 1) * LANES, LANES)] = sign * y[c * n + k]
 
         low = ext.at[fs, pl.ds(PAD, HALO), main]
         high = ext.at[fs, pl.ds(top + rows, HALO), main]
@@ -271,7 +308,8 @@
 
     early_rows = row_start(0, 0, 7)
 
-    keep = keep_ref[...] > 0.0
+    for load in loads[6:]:
+        load.wait()
     n_cat = area_ref.shape[0]
     chunk = 512
 
@@ -448,7 +486,6 @@
     n_slot = n_lon * cap
     wide = cols + LANES
     tall = rows + 2 * HALO
-    pos = curve_pos.astype(jnp.float32)
     ocean = ice_mask > 0
     f32 = functools.partial(pltpu.VMEM, dtype=jnp.float32)
     vmem = pl.BlockSpec(memory_space=pltpu.VMEM)
@@ -459,9 +496,17 @@
             jax.ShapeDtypeStruct(stress.shape, jnp.float32),
             jax.ShapeDtypeStruct((2, n_block, cells), jnp.float32),
         ),
-        in_specs=[vmem] * 12,
+        in_specs=[vmem] * 2 + [pl.BlockSpec(memory_space=pltpu.HBM)] * 9,
         out_specs=(vmem, vmem, vmem),
         scratch_shapes=[
+            f32((rows, cols)),
+            f32((rows, cols)),
+            f32((2, rows, cols)),
+            f32((2, rows, cols)),
+            f32((n_cat, n_block, cells)),
+            f32((n_cat, n_block, cells)),
+            f32((n_block, cells)),
+            pltpu.SemaphoreType.DMA((9,)),
             f32((N_FIELD, tall + 2 * PAD, wide)),
             f32((tall, wide)),
             f32((N_FIELD, HALO, cols)),
@@ -487,11 +532,11 @@
             pltpu.SemaphoreType.DMA((3, n_lon)),
         ],
         compiler_params=pltpu.CompilerParams(
-            collective_id=1, has_side_effects=True, vmem_limit_bytes=48 << 20
+            collective_id=1, has_side_effects=True, vmem_limit_bytes=62 << 20
         ),
         name="coupled",
     )(
-        pos[None, :], pos[:, None], ocean.astype(jnp.float32)[:, None],
+        curve_pos[None, :], ice_mask[None, :],
         surface_temp, salinity, wind_stress, ocean_current, velocity, stress,
         ice_area.transpose(1, 0, 2), ice_volume.transpose(1, 0, 2), air_temp,
     )

time: 101 us -> 93.6 us (0.927)
  local copies, waits for them, and re-layouts: 10.1 us -> 2.41 us
    unnamed x20 -> x12, local copies, waits for them, and re-layouts: 9.96 us -> 2.41 us
    mul x1, other arithmetic: 0.11 us -> 1.24 us  [thermo(): growth = KAPPA * area * (freeze - air)[:, None, :] / (volume + 0.1)]
where the time goes in v3:
time: 93.6 us; the launch traced here: 93.3 us
  Pallas kernels  86.4 us (92%)
  other arithmetic  3.89 us (4%)
  local copies, waits for them, and re-layouts  2.41 us (3%)
    pallas_call x1, Pallas kernels, shards(): pl.pallas_call(functools.partial(coupled_kernel, n_grp, n_lon), out_shape...  86.4 us
    unnamed x12, local copies, waits for them, and re-layouts  2.41 us
    select_n x1, other arithmetic, thermo(): volume_keep = jnp.where(keep, vol_new, volume)  1.99 us

profile of v3, /device:TPU:6, one launch (start us, length us, event | category | flops | bytes accessed | tf_op | source)
XLA Modules:
  0.0 93.3 jit_solution(8283584996559669970)
XLA Ops:
  0.6 0.7 broadcast_compare_fusion
  1.3 0.0 copy-start.2
  1.3 0.0 copy-start.1
  1.3 86.4 %coupled.1 = (f32[2,64,1024]{2,1,0:T(8,128)}, f32[3,64,1024]{2,1,0:T(8,128)}, f32[2,32,2048]{2,1,0:T(8,128)}) custom-call(s32[1,32]{1,0:T(1,128)} %bitcast.21, s32[1,32]{1,0:T(1,128)} %bitcast.22, f32[64,1024]{1,0:T(8,128)} %temp_hbm.1, f32[64,1024]{1,0:T(8,128)} %salt_hbm.1, f32[2,64,1024]{2,1,0:T(8,128)} %wind_hbm.1, f32[2,64,1024]{2,1,0:T(8,128)} %cur_hbm.1, ...), custom_call_target="tpu_custom_call" | custom-call | tf_op jit(solution)/shard_map/coupled/pallas_call | solution.py:492
  87.7 0.0 copy-start
  87.7 0.0 copy-done.2
  87.7 1.2 %fusion = (f32[32,2048]{1,0:T(8,128)S(1)}, f32[32,2048]{1,0:T(8,128)S(1)}, f32[32,2048]{1,0:T(8,128)S(1)}) fusion(f32[32,2048]{1,0:T(8,128)S(1)} %copy-done.2, f32[2,32,2048]{2,1,0:T(8,128)} %get-tuple-element.9), kind=kLoop, calls=%fused_computation.4 | loop fusion | flops 393216 | bytes 1572864 | tf_op jit(solution)/shard_map/mul | solution.py:32
  88.9 0.0 copy-done.1
  88.9 0.2 copy-done
  89.1 0.0 copy-start.4
  89.1 2.0 %multiply_select_fusion.1 = (f32[32,5,2048]{2,0,1:T(8,128)}, f32[32,5,2048]{2,0,1:T(8,128)}) fusion(f32[32,5,2048]{2,0,1:T(8,128)S(1)} %copy-done.1, f32[32,5,2048]{2,0,1:T(8,128)S(1)} %copy-done, f32[32,2048]{1,0:T(8,128)S(1)} %get-tuple-element.13, f32[32,2048]{1,0:T(8,128)S(1)} %get-tuple-element.12, pred[32]{0:T(512)(128)(4,1)S(1)} %broadcast_compare_fusion, ...), kind=kLoop, calls=%fused_computation.1 | loop fusion | flops 2621440 | bytes 6029344 | tf_op jit(solution)/shard_map/jit(_where)/select_n | solution.py:37
  91.1 0.0 copy-start.3
  91.1 0.0 copy-done.4
  91.1 0.8 copy.17
  91.9 0.5 copy-done.3
  92.5 0.9 copy.18
Async XLA Ops:
  1.3 86.4 %copy-start.2 = (f32[32,2048]{1,0:T(8,128)S(1)}, f32[32,2048]{1,0:T(8,128)}, u32[]{:S(2)}) copy-start(f32[32,2048]{1,0:T(8,128)} %air_hbm.1) | copy-start | bytes 786436
  1.3 87.6 %copy-start.1 = (f32[32,5,2048]{2,0,1:T(8,128)S(1)}, f32[32,5,2048]{2,0,1:T(8,128)}, u32[]{:S(2)}) copy-start(f32[32,5,2048]{2,0,1:T(8,128)} %param.18) | copy-start | bytes 3932164
  87.7 1.5 %copy-start = (f32[32,5,2048]{2,0,1:T(8,128)S(1)}, f32[32,5,2048]{2,0,1:T(8,128)}, u32[]{:S(2)}) copy-start(f32[32,5,2048]{2,0,1:T(8,128)} %param.17) | copy-start | bytes 3932164
  89.1 2.0 %copy-start.4 = (f32[2,64,1024]{2,1,0:T(8,128)S(1)}, f32[2,64,1024]{2,1,0:T(8,128)}, u32[]{:S(2)}) copy-start(f32[2,64,1024]{2,1,0:T(8,128)} %get-tuple-element.19) | copy-start | bytes 1572868
  91.1 1.3 %copy-start.3 = (f32[3,64,1024]{2,1,0:T(8,128)S(1)}, f32[3,64,1024]{2,1,0:T(8,128)}, u32[]{:S(2)}) copy-start(f32[3,64,1024]{2,1,0:T(8,128)} %get-tuple-element.20) | copy-start | bytes 2359300

commit v4 on v3

--- a/solution.py
+++ b/solution.py
@@ -113,64 +113,6 @@
     near = sorted(range(1, n_lon), key=lambda d: (min(d, n_lon - d), d))
     far = near[::-1]
 
-    pos_row = pos_ref[...].astype(jnp.float32)
-    down = lax.broadcasted_iota(jnp.int32, (n_block, n_block), 0)
-    along = lax.broadcasted_iota(jnp.int32, (n_block, n_block), 1)
-
-    def column(row):
-        return jnp.sum(jnp.where(down == along, row, 0.0), axis=1, keepdims=True)
-
-    keep = column(mask_ref[...].astype(jnp.float32)) > 0.0
-    to_row = jnp.floor(pos_row * (1.0 / n_block))
-    to_col = column(to_row)
-    same = to_col == to_row
-    rank_row = jnp.sum(jnp.where(same & (down < along), 1.0, 0.0), axis=0, keepdims=True)
-    rank_col = jnp.sum(jnp.where(same & (along < down), 1.0, 0.0), axis=1, keepdims=True)
-    slot_row = to_row * cap + rank_row
-    slot_col = to_col * cap + rank_col
-    slot_down = lax.broadcasted_iota(jnp.int32, (n_slot, n_block), 0).astype(jnp.float32)
-    slot_along = lax.broadcasted_iota(jnp.int32, (n_block, n_slot), 1).astype(jnp.float32)
-    to_slots = jnp.where(slot_down == slot_row, 1.0, 0.0)
-    from_slots = jnp.where(slot_along == slot_col, 1.0, 0.0)
-    pos_slot = jnp.sum(to_slots * (pos_row + 1.0), axis=1, keepdims=True) - 1.0
-    pos_wide = jnp.broadcast_to(pos_slot, (n_slot, LANES))
-    for p in range(n_lon):
-        pos_send[p] = pos_wide[p * cap : (p + 1) * cap]
-
-    loads[0].wait()
-    loads[1].wait()
-    for f, ref in enumerate((temp_ref, salt_ref)):
-        for i in range(rows):
-            for c in range(cols // BX):
-                blocks[f, pl.ds((i // BY) * (cols // BX) + c, 1), pl.ds((i % BY) * BX, BX)] = ref[
-                    pl.ds(i, 1), pl.ds(c * BX, BX)
-                ]
-    for f in range(2):
-        packed = exact_dot(to_slots, blocks[f])
-        for p in range(n_lon):
-            sea_send[p, f] = packed[p * cap : (p + 1) * cap]
-
-    pl.semaphore_wait(
-        barrier, n_lon - 1 + jnp.where(not_south, 1, 0) + jnp.where(not_north, 1, 0)
-    )
-
-    def lon_copy(kind, src, dst, d):
-        return pltpu.make_async_remote_copy(
-            src_ref=src.at[peer(d)], dst_ref=dst.at[l],
-            send_sem=a2a_send.at[kind, d], recv_sem=a2a_recv.at[kind, d],
-            device_id={"grp": g, "lon": peer(d)}, device_id_type=MESH,
-        )
-
-    pos_copy = {d: lon_copy(0, pos_send, pos_recv, d) for d in near}
-    sea_copy = {d: lon_copy(1, sea_send, sea_recv, d) for d in near}
-    ice_copy = {d: lon_copy(2, ice_send, ice_recv, d) for d in near}
-    for d in far:
-        pos_copy[d].start()
-    for d in far:
-        sea_copy[d].start()
-    pos_recv[l] = pos_send[l]
-    sea_recv[l] = sea_send[l]
-
     for load in loads[2:6]:
         load.wait()
     for f in range(2):
@@ -189,6 +131,32 @@
 
     def row_start(part, lo, n):
         fs = pl.ds(lo, n)
+
+        low = ext.at[fs, pl.ds(PAD, HALO), main]
+        high = ext.at[fs, pl.ds(top + rows, HALO), main]
+        to_south = pltpu.make_async_remote_copy(
+            src_ref=ext.at[fs, pl.ds(top, HALO), main], dst_ref=high,
+            send_sem=row_send.at[part, 0], recv_sem=row_recv.at[part, 0],
+            device_id={"grp": jnp.where(not_south, g - 1, g), "lon": l}, device_id_type=MESH,
+        )
+        to_north = pltpu.make_async_remote_copy(
+            src_ref=ext.at[fs, pl.ds(top + rows - HALO, HALO), main], dst_ref=low,
+            send_sem=row_send.at[part, 1], recv_sem=row_recv.at[part, 1],
+            device_id={"grp": jnp.where(not_north, g + 1, g), "lon": l}, device_id_type=MESH,
+        )
+        to_mirror = pltpu.make_async_remote_copy(
+            src_ref=mir.at[fs], dst_ref=high,
+            send_sem=row_send.at[part, 1], recv_sem=row_recv.at[part, 0],
+            device_id={"grp": g, "lon": mirror}, device_id_type=MESH,
+        )
+
+        @pl.when(not_south)
+        def _():
+            to_south.start()
+
+        @pl.when(not_north)
+        def _():
+            to_north.start()
 
         @pl.when(jnp.logical_not(not_north))
         def _():
@@ -216,35 +184,6 @@
                 for k in range(n):
                     sign = -1.0 if lo + k in (0, 1, 5, 6) else 1.0
                     mir[lo + k, :, pl.ds(cols - (c + 1) * LANES, LANES)] = sign * y[c * n + k]
-
-        low = ext.at[fs, pl.ds(PAD, HALO), main]
-        high = ext.at[fs, pl.ds(top + rows, HALO), main]
-        to_south = pltpu.make_async_remote_copy(
-            src_ref=ext.at[fs, pl.ds(top, HALO), main], dst_ref=high,
-            send_sem=row_send.at[part, 0], recv_sem=row_recv.at[part, 0],
-            device_id={"grp": jnp.where(not_south, g - 1, g), "lon": l}, device_id_type=MESH,
-        )
-        to_north = pltpu.make_async_remote_copy(
-            src_ref=ext.at[fs, pl.ds(top + rows - HALO, HALO), main], dst_ref=low,
-            send_sem=row_send.at[part, 1], recv_sem=row_recv.at[part, 1],
-            device_id={"grp": jnp.where(not_north, g + 1, g), "lon": l}, device_id_type=MESH,
-        )
-        to_mirror = pltpu.make_async_remote_copy(
-            src_ref=mir.at[fs], dst_ref=high,
-            send_sem=row_send.at[part, 1], recv_sem=row_recv.at[part, 0],
-            device_id={"grp": g, "lon": mirror}, device_id_type=MESH,
-        )
-
-        @pl.when(not_south)
-        def _():
-            to_south.start()
-
-        @pl.when(not_north)
-        def _():
-            to_north.start()
-
-        @pl.when(jnp.logical_not(not_north))
-        def _():
             to_mirror.start()
 
         return to_south, to_north, to_mirror
@@ -306,7 +245,66 @@
                 lane < HALO, e, jnp.where(lane >= LANES - HALO, w, 0.0)
             )
 
+    pl.semaphore_wait(
+        barrier, n_lon - 1 + jnp.where(not_south, 1, 0) + jnp.where(not_north, 1, 0)
+    )
+
     early_rows = row_start(0, 0, 7)
+
+    pos_row = pos_ref[...].astype(jnp.float32)
+    down = lax.broadcasted_iota(jnp.int32, (n_block, n_block), 0)
+    along = lax.broadcasted_iota(jnp.int32, (n_block, n_block), 1)
+
+    def column(row):
+        return jnp.sum(jnp.where(down == along, row, 0.0), axis=1, keepdims=True)
+
+    keep = column(mask_ref[...].astype(jnp.float32)) > 0.0
+    to_row = jnp.floor(pos_row * (1.0 / n_block))
+    to_col = column(to_row)
+    same = to_col == to_row
+    rank_row = jnp.sum(jnp.where(same & (down < along), 1.0, 0.0), axis=0, keepdims=True)
+    rank_col = jnp.sum(jnp.where(same & (along < down), 1.0, 0.0), axis=1, keepdims=True)
+    slot_row = to_row * cap + rank_row
+    slot_col = to_col * cap + rank_col
+    slot_down = lax.broadcasted_iota(jnp.int32, (n_slot, n_block), 0).astype(jnp.float32)
+    slot_along = lax.broadcasted_iota(jnp.int32, (n_block, n_slot), 1).astype(jnp.float32)
+    to_slots = jnp.where(slot_down == slot_row, 1.0, 0.0)
+    from_slots = jnp.where(slot_along == slot_col, 1.0, 0.0)
+    pos_slot = jnp.sum(to_slots * (pos_row + 1.0), axis=1, keepdims=True) - 1.0
+    pos_wide = jnp.broadcast_to(pos_slot, (n_slot, LANES))
+    for p in range(n_lon):
+        pos_send[p] = pos_wide[p * cap : (p + 1) * cap]
+
+    loads[0].wait()
+    loads[1].wait()
+    for f, ref in enumerate((temp_ref, salt_ref)):
+        for i in range(rows):
+            for c in range(cols // BX):
+                blocks[f, pl.ds((i // BY) * (cols // BX) + c, 1), pl.ds((i % BY) * BX, BX)] = ref[
+                    pl.ds(i, 1), pl.ds(c * BX, BX)
+                ]
+    for f in range(2):
+        packed = exact_dot(to_slots, blocks[f])
+        for p in range(n_lon):
+            sea_send[p, f] = packed[p * cap : (p + 1) * cap]
+
+    def lon_copy(kind, src, dst, d):
+        return pltpu.make_async_remote_copy(
+            src_ref=src.at[peer(d)], dst_ref=dst.at[l],
+            send_sem=a2a_send.at[kind, d], recv_sem=a2a_recv.at[kind, d],
+            device_id={"grp": g, "lon": peer(d)}, device_id_type=MESH,
+        )
+
+    pos_copy = {d: lon_copy(0, pos_send, pos_recv, d) for d in near}
+    sea_copy = {d: lon_copy(1, sea_send, sea_recv, d) for d in near}
+    ice_copy = {d: lon_copy(2, ice_send, ice_recv, d) for d in near}
+    for d in far:
+        pos_copy[d].start()
+    for d in far:
+        sea_copy[d].start()
+    pos_recv[l] = pos_send[l]
+    sea_recv[l] = sea_send[l]
+
 
     for load in loads[6:]:
         load.wait()

time: 93.6 us -> 91.5 us (0.978)
  Pallas kernels: 86.4 us -> 84.3 us
    pallas_call x1, Pallas kernels: 86.4 us -> 84.3 us  [shards(): pl.pallas_call(functools.partial(coupled_kernel, n_grp, n_lon), out_shape...]
where the time goes in v4:
time: 91.5 us; the launch traced here: 91.2 us
  Pallas kernels  84.3 us (92%)
  other arithmetic  3.89 us (4%)
  local copies, waits for them, and re-layouts  2.41 us (3%)
    pallas_call x1, Pallas kernels, shards(): pl.pallas_call(functools.partial(coupled_kernel, n_grp, n_lon), out_shape...  84.3 us
    unnamed x12, local copies, waits for them, and re-layouts  2.41 us
    select_n x1, other arithmetic, thermo(): volume_keep = jnp.where(keep, vol_new, volume)  1.99 us

profile of v4, /device:TPU:6, one launch (start us, length us, event | category | flops | bytes accessed | tf_op | source)
XLA Modules:
  0.0 91.2 jit_solution(4308015134248218515)
XLA Ops:
  0.6 0.7 broadcast_compare_fusion
  1.3 0.0 copy-start.2
  1.3 0.0 copy-start.1
  1.3 84.3 %coupled.1 = (f32[2,64,1024]{2,1,0:T(8,128)}, f32[3,64,1024]{2,1,0:T(8,128)}, f32[2,32,2048]{2,1,0:T(8,128)}) custom-call(s32[1,32]{1,0:T(1,128)} %bitcast.21, s32[1,32]{1,0:T(1,128)} %bitcast.22, f32[64,1024]{1,0:T(8,128)} %temp_hbm.1, f32[64,1024]{1,0:T(8,128)} %salt_hbm.1, f32[2,64,1024]{2,1,0:T(8,128)} %wind_hbm.1, f32[2,64,1024]{2,1,0:T(8,128)} %cur_hbm.1, ...), custom_call_target="tpu_custom_call" | custom-call | tf_op jit(solution)/shard_map/coupled/pallas_call | solution.py:490
  85.6 0.0 copy-start
  85.6 0.0 copy-done.2
  85.6 1.2 %fusion = (f32[32,2048]{1,0:T(8,128)S(1)}, f32[32,2048]{1,0:T(8,128)S(1)}, f32[32,2048]{1,0:T(8,128)S(1)}) fusion(f32[32,2048]{1,0:T(8,128)S(1)} %copy-done.2, f32[2,32,2048]{2,1,0:T(8,128)} %get-tuple-element.9), kind=kLoop, calls=%fused_computation.4 | loop fusion | flops 393216 | bytes 1572864 | tf_op jit(solution)/shard_map/mul | solution.py:32
  86.8 0.0 copy-done.1
  86.8 0.2 copy-done
  87.0 0.0 copy-start.4
  87.0 2.0 %multiply_select_fusion.1 = (f32[32,5,2048]{2,0,1:T(8,128)}, f32[32,5,2048]{2,0,1:T(8,128)}) fusion(f32[32,5,2048]{2,0,1:T(8,128)S(1)} %copy-done.1, f32[32,5,2048]{2,0,1:T(8,128)S(1)} %copy-done, f32[32,2048]{1,0:T(8,128)S(1)} %get-tuple-element.13, f32[32,2048]{1,0:T(8,128)S(1)} %get-tuple-element.12, pred[32]{0:T(512)(128)(4,1)S(1)} %broadcast_compare_fusion, ...), kind=kLoop, calls=%fused_computation.1 | loop fusion | flops 2621440 | bytes 6029344 | tf_op jit(solution)/shard_map/jit(_where)/select_n | solution.py:37
  89.0 0.0 copy-start.3
  89.0 0.0 copy-done.4
  89.0 0.8 copy.17
  89.8 0.5 copy-done.3
  90.4 0.9 copy.18
Async XLA Ops:
  1.3 84.3 %copy-start.2 = (f32[32,2048]{1,0:T(8,128)S(1)}, f32[32,2048]{1,0:T(8,128)}, u32[]{:S(2)}) copy-start(f32[32,2048]{1,0:T(8,128)} %air_hbm.1) | copy-start | bytes 786436
  1.3 85.5 %copy-start.1 = (f32[32,5,2048]{2,0,1:T(8,128)S(1)}, f32[32,5,2048]{2,0,1:T(8,128)}, u32[]{:S(2)}) copy-start(f32[32,5,2048]{2,0,1:T(8,128)} %param.18) | copy-start | bytes 3932164
  85.6 1.5 %copy-start = (f32[32,5,2048]{2,0,1:T(8,128)S(1)}, f32[32,5,2048]{2,0,1:T(8,128)}, u32[]{:S(2)}) copy-start(f32[32,5,2048]{2,0,1:T(8,128)} %param.17) | copy-start | bytes 3932164
  87.0 2.0 %copy-start.4 = (f32[2,64,1024]{2,1,0:T(8,128)S(1)}, f32[2,64,1024]{2,1,0:T(8,128)}, u32[]{:S(2)}) copy-start(f32[2,64,1024]{2,1,0:T(8,128)} %get-tuple-element.19) | copy-start | bytes 1572868
  89.0 1.3 %copy-start.3 = (f32[3,64,1024]{2,1,0:T(8,128)S(1)}, f32[3,64,1024]{2,1,0:T(8,128)}, u32[]{:S(2)}) copy-start(f32[3,64,1024]{2,1,0:T(8,128)} %get-tuple-element.20) | copy-start | bytes 2359300
